TPU v7x, 1024 devices: a whole 4x4x32 slice. The times are simulated.
1024 devices in a mesh: ctx: 16 (over y, x), tp: 64 (over z, core).
Axes of the slice: x: 4, y: 4, z: 32, core: 2. Of those that a mesh axis runs over, the one named last changes fastest.
Arguments:
- short_query: bfloat16 [4096, 32768], P('tp', 'ctx'), may hold values from -16 to 16
- short_key: bfloat16 [4096, 32768], P('tp', 'ctx'), may hold values from -6 to 6
- short_value: bfloat16 [4096, 32768], P('tp', 'ctx'), may hold values from -6 to 6
- short_taps: bfloat16 [4096, 128], P('tp'), may hold values from -0.5 to 0.5
- norm_gain: float32 [4096], P('tp'), may hold values from 0.1 to 1.9
- long_key: bfloat16 [4096, 32768], P('tp', 'ctx'), may hold values from -6 to 6
- long_query: bfloat16 [4096, 32768], P('tp', 'ctx'), may hold values from -6 to 6
- residues: float32 [16, 4096], P(None, 'tp'), may hold values from -1.5 to 1.5
- decay_rates: float32 [16, 4096], P(None, 'tp'), may hold values from 1.5258789e-05 to 0.05
Outputs:
- mixer_output: float32 [4096, 32768], P('tp', 'ctx')
All inputs are finite; a program needn't handle non-finite values.
Results may differ from a plain program's by a relative error of at most 0.0029.
Values may be sent and summed in bfloat16 or wider, within the bound.
No kernel may reach another device: no remote copies, remote signals or barrier semaphores. Data moves between devices by JAX's collectives and lax.ppermute only.
A program may use at most 64 MiB of HBM per device.

v0:
```python
import functools

import jax
import jax.numpy as jnp
from jax import lax
from jax.sharding import Mesh
from jax.sharding import PartitionSpec as P

D = 4096
TP = ("tp_0", "tp_1")


highest = lax.Precision.HIGHEST


def passed_along(value, axis, by):
    devices = lax.axis_size(axis)
    pairs = [(i, i + by) for i in range(devices) if 0 <= i + by < devices]
    return lax.ppermute(value, axis, pairs)


def by_axis(value, axes):
    return functools.reduce(lax.psum, axes, value)


def make_band(filter_taps):
    tap_count = filter_taps.shape[1]
    row_index = jnp.arange(tap_count)[:, None]
    col_index = jnp.arange(2 * tap_count)[None, :]
    lag_index = row_index + tap_count - col_index
    inside = (lag_index >= 0) & (lag_index < tap_count)
    picked = jnp.take(filter_taps, jnp.clip(lag_index, 0, tap_count - 1), axis=1)
    return jnp.where(inside[None, :, :], picked, jnp.zeros_like(picked))


def short_block(extended, filter_taps):
    tap_count = filter_taps.shape[1]
    channels, span_len = extended.shape
    length = span_len - tap_count
    block_count = length // tap_count
    earlier = extended[:, :length].reshape(channels, block_count, tap_count)
    current = extended[:, tap_count:].reshape(channels, block_count, tap_count)
    windows = jnp.concatenate([earlier, current], axis=2)
    band_rows = make_band(filter_taps)
    mixed = jnp.einsum("cbm,cim->cbi", windows, band_rows, preferred_element_type=jnp.float32)
    return mixed.reshape(channels, length)


def response(residue, decays, outer_len, length):
    full_len = 2 * length
    frequency = jnp.arange(outer_len)[:, None] + outer_len * jnp.arange(256)[None, :]
    angles = 2.0 * jnp.pi / full_len * frequency.astype(jnp.float32)
    parity = 1.0 - 2.0 * (frequency % 2).astype(jnp.float32)
    decay_grid = decays[:, :, None, None]
    ratios = jnp.exp(-decay_grid)
    weights = (residue * jnp.sqrt(-jnp.expm1(-2.0 * decays)))[:, :, None, None]
    half_sine = jnp.sin(0.5 * angles)
    real_den = -jnp.expm1(-decay_grid) + 2.0 * ratios * half_sine * half_sine
    imag_den = ratios * jnp.sin(angles)
    scaled = (
        weights
        * (1.0 - jnp.exp(-decay_grid * length) * parity)
        / (real_den * real_den + imag_den * imag_den)
    )
    return (jnp.sum(scaled * real_den, axis=0), jnp.sum(-scaled * imag_den, axis=0))


def spectral_mix(signal, residue, decays):
    channels, length = signal.shape
    full_len = 2 * length
    outer_len = full_len // 256
    half_len = outer_len // 2
    row_index = jnp.arange(half_len)[:, None]
    col_index = jnp.arange(outer_len)[None, :]
    angles = 2.0 * jnp.pi / outer_len * (row_index * col_index % outer_len).astype(jnp.float32)
    first_table = jnp.concatenate([jnp.cos(angles), -jnp.sin(angles)], axis=1)
    last_table = jnp.concatenate([jnp.cos(angles).T, -jnp.sin(angles).T], axis=0)
    twist_phase = jnp.arange(outer_len)[:, None] * jnp.arange(256)[None, :] % full_len
    twist_angle = 2.0 * jnp.pi / full_len * twist_phase.astype(jnp.float32)
    twist_cos = jnp.cos(twist_angle)
    twist_sin = jnp.sin(twist_angle)
    inner_phase = jnp.arange(256)[:, None] * jnp.arange(256)[None, :] % 256
    inner_angle = 2.0 * jnp.pi / 256 * inner_phase.astype(jnp.float32)
    inner_cos = jnp.cos(inner_angle)
    inner_sin = jnp.sin(inner_angle)
    inner_table = jnp.concatenate(
        [
            jnp.concatenate([inner_cos, -inner_sin], axis=1),
            jnp.concatenate([inner_sin, inner_cos], axis=1),
        ],
        axis=0,
    )
    resp_real, resp_imag = response(residue, decays, outer_len, length)
    grid = signal.reshape(channels, half_len, 256)
    stacked = jnp.einsum("kab,ae->keb", grid, first_table, precision=highest)
    real_first = stacked[:, :outer_len]
    imag_first = stacked[:, outer_len:]
    real_twist = real_first * twist_cos + imag_first * twist_sin
    imag_twist = imag_first * twist_cos - real_first * twist_sin
    joined = jnp.concatenate([real_twist, imag_twist], axis=2)
    spectrum = jnp.einsum("kcm,mn->kcn", joined, inner_table, precision=highest)
    real_spec = spectrum[:, :, :256]
    imag_spec = spectrum[:, :, 256:]
    real_prod = real_spec * resp_real - imag_spec * resp_imag
    imag_prod = real_spec * resp_imag + imag_spec * resp_real
    inverse = jnp.einsum(
        "kcm,mn->kcn",
        jnp.concatenate([real_prod, imag_prod], axis=2),
        inner_table.T,
        precision=highest,
    )
    real_back = inverse[:, :, :256]
    imag_back = inverse[:, :, 256:]
    real_turn = real_back * twist_cos - imag_back * twist_sin
    imag_turn = imag_back * twist_cos + real_back * twist_sin
    result = jnp.einsum(
        "keb,ea->kab",
        jnp.concatenate([real_turn, imag_turn], axis=1),
        last_table,
        precision=highest,
    )
    return result.reshape(channels, length) / full_len


def shards(
    short_query,
    short_key,
    short_value,
    short_taps,
    norm_gain,
    long_key,
    long_query,
    residues,
    decay_rates,
):
    tap_count = short_taps.shape[1]
    channels, local_len = short_value.shape
    first_product = (short_key.astype(jnp.float32) * short_value.astype(jnp.float32)).astype(
        jnp.bfloat16
    )
    previous = passed_along(first_product[:, local_len - tap_count :], "ctx", 1)
    extended = jnp.concatenate([previous, first_product], axis=1)
    short_mix = short_block(extended, short_taps)
    gated = short_query.astype(jnp.float32) * short_mix
    squares = by_axis(jnp.sum(gated * gated, axis=0), TP)
    normed = gated * norm_gain[:, None] * lax.rsqrt(squares / D + 1e-06)[None, :]
    long_input = long_key.astype(jnp.float32) * normed
    own_count = channels // lax.axis_size("ctx")
    regrouped = lax.all_to_all(long_input, "ctx", split_axis=0, concat_axis=1, tiled=True)
    first_channel = lax.axis_index("ctx") * own_count
    own_residue = lax.dynamic_slice_in_dim(residues, first_channel, own_count, 1)
    own_decay = lax.dynamic_slice_in_dim(decay_rates, first_channel, own_count, 1)
    mixed_whole = spectral_mix(regrouped, own_residue, own_decay)
    long_mix = lax.all_to_all(mixed_whole, "ctx", split_axis=1, concat_axis=0, tiled=True)
    return long_query.astype(jnp.float32) * long_mix


def solution(mesh):
    split = Mesh(mesh.devices.reshape(mesh.shape["ctx"], 32, 2), ("ctx", "tp_0", "tp_1"))
    in_specs = (
        P(TP, "ctx"),
        P(TP, "ctx"),
        P(TP, "ctx"),
        P(TP, None),
        P(TP),
        P(TP, "ctx"),
        P(TP, "ctx"),
        P(None, TP),
        P(None, TP),
    )
    out_specs = P(TP, "ctx")
    return jax.shard_map(
        shards, mesh=split, in_specs=in_specs, out_specs=out_specs, check_vma=False
    )
```

profile of v0, /device:TPU:1, one launch (start us, length us, event | category | flops | bytes accessed | tf_op | source)
XLA Modules:
  0.0 274.1 jit_solution(9872998565117585125)
XLA Ops:
  0.0 1.1 multiply_convert_fusion
  1.1 3.9 %collective-permute-start = (bf16[64,128]{1,0:T(8,128)(2,1)S(1)}, bf16[64,128]{1,0:T(8,128)(2,1)S(1)}, u32[]{:S(2)}, u32[]{:S(2)}) collective-permute-start(bf16[64,128]{1,0:T(8,128)(2,1)S(1)} %slice.34), channel_id=1, source_target_pairs={{0,64},{64,128},{128,192},{192,256},{256,320},{320,384},{384,448},... | collective-permute-start | bytes 49160 | tf_op jit(solution)/shard_map/ppermute | solution.py:19
  5.5 1.8 fusion.39
  8.1 10.4 %fusion.2 = (f32[4,256,256]{2,1,0:T(8,128)S(1)}, f32[4,256,256]{2,1,0:T(8,128)S(1)}) fusion(f32[256,256]{1,0:T(8,128)S(1)} %get-tuple-element.21, f32[16,4]{1,0:T(8,128)S(1)} %get-tuple-element.18, f32[256,256]{1,0:T(8,128)S(1)} %get-tuple-element.22, f32[16,4]{1,0:T(8,128)S(1)} %get-tuple-element.17, f32[16,4]{1,0:T(8,128)S(1)} %get-tuple-element.16, ...), kind=kLoop, calls=%fused_computation.5 | loop fusion | flops 66584576 | bytes 2884864 | tf_op jit(solution)/shard_map/reduce_sum | solution.py:65
  18.5 1.7 fusion.65
  20.3 114.2 %gather_fusion = bf16[32768,64]{1,0:T(8,128)(2,1)} fusion(bf16[64,128]{0,1:T(8,128)(2,1)S(1)} %copy.41, s32[32768]{0:T(1024)S(1)} %broadcast_clamp_fusion), kind=kCustom, calls=%fused_computation | custom fusion | bytes 8519680 | tf_op jit(solution)/shard_map/jit(_take)/gather | solution.py:32
  134.5 10.1 %copy.42 = bf16[128,256,64]{1,0,2:T(8,128)(2,1)} copy(bf16[128,256,64]{2,1,0:T(8,128)(2,1)} %bitcast.37) | data formatting | bytes 8388608 | tf_op jit(solution)/shard_map/jit(_take)/gather | solution.py:32
  144.7 3.4 %fusion.3 = f32[64,16,128]{2,1,0:T(8,128)S(1)} fusion(bf16[128,256,64]{1,0,2:T(8,128)(2,1)} %copy.42, pred[128,256]{1,0:T(8,128)(4,1)S(1)} %get-tuple-element.24, pred[128,256]{1,0:T(8,128)(4,1)S(1)} %get-tuple-element.23, bf16[64,16,128]{2,1,0:T(8,128)(2,1)S(1)} %bitcast.43, bf16[64,16,128]{2,1,0:T(8,128)(2,1)S(1)} %bitcast.44), kind=kOutput, calls=%fused_computation.8 | convolution fusion | flops 72351744 | bytes 5308416 | tf_op jit(solution)/shard_map/cbm,cim->cbi/dot_general | solution.py:45
  148.3 56.4 %psum.14 = f32[2048]{0:T(1024)S(1)} all-reduce(f32[2048]{0:T(1024)S(1)} %multiply_reduce_fusion.1), channel_id=1, replica_groups=mesh['ctx'=16,'tp_0'=32,'tp_1'=2] {'tp_0'}, use_global_device_ids=true, to_apply=%region_1.2 | all-reduce | flops 2048 | bytes 16384 | tf_op jit(solution)/shard_map/psum | solution.py:23
  204.7 17.2 %psum.15 = f32[2048]{0:T(1024)S(1)} all-reduce(f32[2048]{0:T(1024)S(1)} %psum.14), channel_id=1, replica_groups=mesh['ctx'=16,'tp_0'=32,'tp_1'=2] {'tp_1'}, use_global_device_ids=true, to_apply=%region_2.3 | all-reduce | flops 2048 | bytes 16384 | tf_op jit(solution)/shard_map/psum | solution.py:23
  222.0 1.2 multiply_multiply_fusion.2
  224.1 6.7 %all-to-all-start = ((f32[16,4,2048]{2,1,0:T(4,128)}), f32[16,4,2048]{2,1,0:T(4,128)}, u32[]{:S(2)}, u32[]{:S(2)}) async-start(f32[16,4,2048]{2,1,0:T(4,128)} %all_to_all.24), calls=%async_computation | async-start | bytes 1048576 | tf_op jit(solution)/shard_map/all_to_all | solution.py:149
  231.8 1.1 copy.45
  233.0 1.2 sine_negate_fusion
  235.2 1.2 sine_negate_fusion.1
  236.4 1.0 fusion.62
  237.5 4.0 %all-to-all-done = f32[16,4,2048]{2,1,0:T(4,128)} async-done(((f32[16,4,2048]{2,1,0:T(4,128)}), f32[16,4,2048]{2,1,0:T(4,128)}, u32[]{:S(2)}, u32[]{:S(2)}) %all-to-all-start) | async-done | bytes 524320 | tf_op jit(solution)/shard_map/all_to_all | solution.py:149
  241.5 2.1 copy.43
  243.6 1.9 reshape.243
  245.5 3.0 %convolution_bitcast_fusion = f32[4,512,256]{1,2,0:T(8,128)S(1)} fusion(f32[4,128,256]{2,1,0:T(8,128)} %reshape.243, f32[128,256]{1,0:T(8,128)} %get-tuple-element.25, f32[128,256]{1,0:T(8,128)} %get-tuple-element.26), kind=kOutput, calls=%fused_computation.28 | convolution fusion | flops 805371904 | bytes 2883584 | tf_op jit(solution)/shard_map/kab,ae->keb/dot_general | solution.py:95
  248.8 3.5 %fusion.9 = f32[4,256,512]{2,1,0:T(8,128)S(1)} fusion(f32[4,256,256]{1,2,0:T(8,128)S(1)} %get-tuple-element.14, f32[4,256,256]{1,2,0:T(8,128)S(1)} %get-tuple-element.13, f32[256,256]{1,0:T(8,128)S(1)} %get-tuple-element.28, f32[256,256]{1,0:T(8,128)S(1)} %get-tuple-element.27, f32[256,256]{1,0:T(8,128)S(1)} %fusion.78), kind=kOutput, calls=%fused_computation.14 | convolution fusion | flops 3222536192 | bytes 4980736 | tf_op jit(solution)/shard_map/kcm,mn->kcn/dot_general | solution.py:101
  252.8 3.8 %fusion.13 = f32[4,256,512]{1,2,0:T(8,128)S(1)} fusion(f32[4,256,256]{2,1,0:T(8,128)S(1)} %get-tuple-element.10, f32[4,256,256]{2,1,0:T(8,128)S(1)} %get-tuple-element.9, f32[256,256]{1,0:T(8,128)S(1)} %get-tuple-element.28, f32[256,256]{1,0:T(8,128)S(1)} %get-tuple-element.27, f32[256,256]{1,0:T(8,128)S(1)} %fusion.78), kind=kOutput, calls=%fused_computation.18 | convolution fusion | flops 3222536192 | bytes 4980736 | tf_op jit(solution)/shard_map/kcm,mn->kcn/dot_general | solution.py:106
  256.9 2.3 fusion.26
  259.6 13.5 %all_to_all.32 = f32[4,16,2048]{2,0,1:T(4,128)S(1)} all-to-all(f32[4,16,2048]{2,0,1:T(4,128)S(1)} %copy.51), channel_id=1, replica_groups=mesh['ctx'=16,'tp_0'=32,'tp_1'=2] {'ctx'}, dimensions={1} | all-to-all | bytes 1048576 | tf_op jit(solution)/shard_map/all_to_all | solution.py:154
  (36 shorter events, 7.1 us)
Async XLA Ops:
  0.0 20.2 %copy-start.3 = (bf16[64,128]{1,0:T(8,128)(2,1)S(1)}, bf16[64,128]{1,0:T(8,128)(2,1)}, u32[]{:S(2)}) copy-start(bf16[64,128]{1,0:T(8,128)(2,1)} %param.12) | copy-start | bytes 49156
  1.1 143.5 %collective-permute-start = (bf16[64,128]{1,0:T(8,128)(2,1)S(1)}, bf16[64,128]{1,0:T(8,128)(2,1)S(1)}, u32[]{:S(2)}, u32[]{:S(2)}) collective-permute-start(bf16[64,128]{1,0:T(8,128)(2,1)S(1)} %slice.34), channel_id=1, source_target_pairs={{0,64},{64,128},{128,192},{192,256},{256,320},{320,384},{384,448},... | collective-permute-start | bytes 49160 | tf_op jit(solution)/shard_map/ppermute | solution.py:19
  144.7 3.4 %copy-start = (bf16[64,2048]{1,0:T(8,128)(2,1)S(1)}, bf16[64,2048]{1,0:T(8,128)(2,1)}, u32[]{:S(2)}) copy-start(bf16[64,2048]{1,0:T(8,128)(2,1)} %param.9) | copy-start | bytes 786436
  144.7 77.3 %copy-start.4 = (f32[64]{0:T(128)S(1)}, f32[64]{0:T(128)}, u32[]{:S(2)}) copy-start(f32[64]{0:T(128)} %param.13) | copy-start | bytes 772
  224.1 17.3 %all-to-all-start = ((f32[16,4,2048]{2,1,0:T(4,128)}), f32[16,4,2048]{2,1,0:T(4,128)}, u32[]{:S(2)}, u32[]{:S(2)}) async-start(f32[16,4,2048]{2,1,0:T(4,128)} %all_to_all.24), calls=%async_computation | async-start | bytes 1048576 | tf_op jit(solution)/shard_map/all_to_all | solution.py:149
  252.8 4.1 %copy-start.1 = (f32[256,128]{0,1:T(8,128)S(1)}, f32[256,128]{0,1:T(8,128)}, u32[]{:S(2)}) copy-start(f32[256,128]{0,1:T(8,128)} %get-tuple-element.30) | copy-start | bytes 393220
  256.9 16.4 %copy-start.2 = (bf16[64,2048]{1,0:T(8,128)(2,1)S(1)}, bf16[64,2048]{1,0:T(8,128)(2,1)}, u32[]{:S(2)}) copy-start(bf16[64,2048]{1,0:T(8,128)(2,1)} %param.15) | copy-start | bytes 786436
where the time goes:
time: 275 us; the launch traced here: 274 us
  local copies, waits for them, and re-layouts  131 us (48%)
  blocking collectives  87.1 us (32%)
  other arithmetic  24.7 us (9%)
  matrix products  16 us (6%)
  starting transfers between devices  10.6 us (4%)
  waiting for transfers between devices  4 us (1%)
    gather x2, local copies, waits for them, and re-layouts, make_band(): jnp.take(filter_taps, jnp.clip(lag_index, 0, tap_count - 1), axis=1)  124 us
    psum x2, blocking collectives, by_axis(): return functools.reduce(lax.psum, axes, value)  73.6 us
    all_to_all x1, blocking collectives, shards(): lax.all_to_all(mixed_whole, 'ctx', split_axis=1, concat_axis=0, tiled=True)  13.5 us
    reduce_sum x1, other arithmetic, response(): jnp.sum(-scaled * imag_den, axis=0)  10.4 us
    all_to_all x1, starting transfers between devices, shards(): lax.all_to_all(long_input, 'ctx', split_axis=0, concat_axis=1, tiled=True)  6.7 us
  transfers between devices with their start and end apart: 2, of which 1 were waited for; matrix products, arithmetic and copies ran while one was open for 53% of the time, Pallas kernels for 0%

commit v1 on v0

v1 whole, which is shorter than its diff:
```python
import jax
import jax.numpy as jnp
from jax import lax
from jax.experimental import pallas as pl
from jax.experimental.pallas import tpu as pltpu
from jax.sharding import Mesh
from jax.sharding import PartitionSpec as P

D = 4096
TP = ("z", "core")
BLOCK = 128
GROUP = 8
UNROLL = 32
PARTS = 2
INTERPRET = False
f32 = jnp.float32
bf16 = jnp.bfloat16


def call(kernel, out_shape, in_specs, out_specs, scratch=(), flops=0, bytes_accessed=0, limit=40 << 20):
    return pl.pallas_call(
        kernel,
        out_shape=out_shape,
        in_specs=in_specs,
        out_specs=out_specs,
        scratch_shapes=list(scratch),
        compiler_params=pltpu.CompilerParams(vmem_limit_bytes=limit),
        cost_estimate=pl.CostEstimate(
            flops=flops, bytes_accessed=bytes_accessed, transcendentals=0
        ),
        interpret=INTERPRET,
    )


def halves(value):
    high = value.astype(bf16)
    return high, (value - high.astype(f32)).astype(bf16)


def circulant(row):
    spread = jnp.broadcast_to(row, (BLOCK, BLOCK))
    return pltpu.roll(spread, 0, 1, stride=1, stride_axis=0)


def dot(left, right):
    return lax.dot_general(
        left, right, (((1,), (0,)), ((), ())), preferred_element_type=f32
    )


def dot_nt(left, right):
    return lax.dot_general(
        left, right, (((1,), (1,)), ((), ())), preferred_element_type=f32
    )


def upper_mask():
    row = lax.broadcasted_iota(jnp.int32, (BLOCK, BLOCK), 0)
    lane = lax.broadcasted_iota(jnp.int32, (BLOCK, BLOCK), 1)
    return lane >= row


def own_lanes():
    row = lax.broadcasted_iota(jnp.int32, (GROUP, BLOCK), 0)
    lane = lax.broadcasted_iota(jnp.int32, (GROUP, BLOCK), 1)
    return lane % GROUP == row


def short_kernel(
    taps_hbm, key_hbm, value_hbm, mixed_ref, last_ref,
    taps_ref, key_ref, value_ref, taps, xs, ps, sems,
):
    channels, length = key_ref.shape
    blocks = length // BLOCK
    part = channels // PARTS
    first = pltpu.make_async_copy(taps_hbm, taps_ref, sems.at[2 * PARTS])
    first.start()
    copies = []
    for i in range(PARTS):
        rows = pl.ds(i * part, part)
        pair = [
            pltpu.make_async_copy(source.at[rows], target.at[rows], sems.at[2 * i + k])
            for k, (source, target) in enumerate(
                ((key_hbm, key_ref), (value_hbm, value_ref))
            )
        ]
        for copy in pair:
            copy.start()
        copies.append(pair)
    upper = upper_mask()

    def one(c, carry):
        ring = circulant(taps[pl.ds(c, 1), :])
        zero = jnp.zeros_like(ring)
        band = jnp.concatenate(
            [jnp.where(upper, ring, zero), jnp.where(upper, zero, ring)], axis=1
        ).astype(bf16)
        both = dot(xs[pl.ds(c, blocks, stride=channels), :].astype(bf16), band)
        mixed_ref[pl.ds(c, blocks, stride=channels), :] = both[:, :BLOCK]
        ps[pl.ds(c + channels, blocks, stride=channels), :] = both[:, BLOCK:]
        return carry

    first.wait()
    taps[...] = taps_ref[...].astype(f32)
    for i in range(PARTS):
        for copy in copies[i]:
            copy.wait()
        own = slice(i * part, (i + 1) * part)
        for b in range(blocks):
            cols = slice(b * BLOCK, (b + 1) * BLOCK)
            at = b * channels + i * part
            xs[at : at + part, :] = key_ref[own, cols].astype(f32) * value_ref[
                own, cols
            ].astype(f32)
        lax.fori_loop(i * part, (i + 1) * part, one, 0, unroll=UNROLL)
    last_ref[...] = ps[blocks * channels :, :]
    mixed_ref[channels:, :] += ps[channels : blocks * channels, :]


def gate_kernel(
    taps_ref, gain_ref, query_hbm, key_hbm,
    mixed_ref, squares_ref, open_mix, open_query, open_key, query_ref, key_ref, sems,
):
    copies = [
        pltpu.make_async_copy(query_hbm, query_ref, sems.at[0]),
        pltpu.make_async_copy(key_hbm, key_ref, sems.at[1]),
    ]
    for copy in copies:
        copy.start()
    channels, length = query_ref.shape
    blocks = length // BLOCK
    row = lax.broadcasted_iota(jnp.int32, (channels, channels), 0)
    lane = lax.broadcasted_iota(jnp.int32, (channels, channels), 1)
    spread = jnp.broadcast_to(gain_ref[...], (channels, channels))
    gain = jnp.sum(jnp.where(row == lane, spread, 0.0), axis=1, keepdims=True)
    for copy in copies:
        copy.wait()
    open_query[...] = query_ref[:, :BLOCK].astype(f32)
    open_key[...] = gain * key_ref[:, :BLOCK].astype(f32)
    open_mix[...] = taps_ref[:channels, :]
    mixed_ref[:channels, :] = jnp.zeros((channels, BLOCK), f32)
    squares_ref[0:1, :] = jnp.zeros((1, BLOCK), f32)
    for b in range(1, blocks):
        cols = slice(b * BLOCK, (b + 1) * BLOCK)
        rows = slice(b * channels, (b + 1) * channels)
        gated = query_ref[:, cols].astype(f32) * taps_ref[rows, :]
        squares_ref[b : b + 1, :] = jnp.sum(gated * gated, axis=0, keepdims=True)
        mixed_ref[rows, :] = gated * gain * key_ref[:, cols].astype(f32)


def table_kernel(decay_ref, weight_ref, into_hi, into_lo, out_hi, out_lo, long_taps_ref):
    groups = decay_ref.shape[1]
    lane = lax.broadcasted_iota(jnp.int32, (1, BLOCK), 1).astype(f32)
    for g in range(groups):
        rows = slice(g * BLOCK, (g + 1) * BLOCK)
        decay = decay_ref[:, g : g + 1]
        weight = weight_ref[:, g : g + 1]
        into_hi[rows, :], into_lo[rows, :] = halves(jnp.exp(-decay * (BLOCK - lane)))
        out = weight * jnp.exp(-decay * lane)
        out_hi[rows, :], out_lo[rows, :] = halves(out)
        long_taps_ref[g * GROUP : (g + 1) * GROUP, :] = jnp.sum(
            out.reshape(BLOCK // GROUP, GROUP, BLOCK), axis=0
        )


def join_kernel(short_ref, halo_ref, query_ref, key_ref, rest_ref, mixed_ref, squares_ref):
    gated = query_ref[...] * (short_ref[...] + halo_ref[...])
    squares_ref[...] = rest_ref[...]
    squares_ref[0:1, :] = jnp.sum(gated * gated, axis=0, keepdims=True)
    mixed_ref[...] = gated * key_ref[...]


def state_kernel(
    first_ref, mixed_ref, squares_ref, into_hi, into_lo, decay_ref,
    signal_ref, states_ref, last_ref,
):
    groups = decay_ref.shape[0]
    channels = groups * GROUP
    blocks = mixed_ref.shape[0] // channels
    own = own_lanes()
    scales = lax.rsqrt(squares_ref[...] / D + 1e-06)
    signal_ref[:channels, :] = first_ref[...] * scales[0:1, :]
    for b in range(1, blocks):
        rows = slice(b * channels, (b + 1) * channels)
        signal_ref[rows, :] = mixed_ref[rows, :] * scales[b : b + 1, :]
    for g in range(groups):
        rows = slice(g * BLOCK, (g + 1) * BLOCK)
        left = jnp.concatenate(
            [
                signal_ref[b * channels + g * GROUP : b * channels + (g + 1) * GROUP, :]
                for b in range(blocks)
            ],
            axis=0,
        )
        hi, lo = halves(left)
        wide = dot_nt(jnp.concatenate([hi, lo], axis=0), into_hi[rows, :])
        size = left.shape[0]
        added = wide[:size] + wide[size:] + dot_nt(hi, into_lo[rows, :])
        fade = jnp.exp(-float(BLOCK) * decay_ref[g : g + 1, :])
        state = jnp.zeros((GROUP, BLOCK), f32)
        for b in range(blocks):
            place = g * size + b * GROUP
            states_ref[place : place + GROUP, :] = state
            state = fade * state + jnp.where(own, added[b * GROUP : (b + 1) * GROUP], 0.0)
        end = jnp.sum(state, axis=0, keepdims=True)
        for j in range(last_ref.shape[0]):
            last_ref[j, g : g + 1, :] = end


def within_kernel(signal_ref, taps_ref, result_ref):
    channels = taps_ref.shape[0]
    blocks = signal_ref.shape[0] // channels
    upper = upper_mask()

    def one(c, carry):
        ring = circulant(taps_ref[pl.ds(c, 1), :])
        hi_band, lo_band = halves(jnp.where(upper, ring, 0.0))
        hi, lo = halves(signal_ref[pl.ds(c, blocks, stride=channels), :])
        wide = dot(jnp.concatenate([hi, lo], axis=0), hi_band)
        total = wide[:blocks] + wide[blocks:] + dot(hi, lo_band)
        result_ref[pl.ds(c, blocks, stride=channels), :] = total
        return carry

    lax.fori_loop(0, channels, one, 0, unroll=UNROLL)


def finish_kernel(
    index_ref, within_ref, states_ref, last_ref, out_hi, out_lo, decay_ref,
    long_query_ref, result_ref, ys,
):
    groups = decay_ref.shape[0]
    channels = groups * GROUP
    blocks = within_ref.shape[0] // channels
    length = blocks * BLOCK
    own = own_lanes()
    place = index_ref[0]
    decay = decay_ref[...]
    carry = jnp.zeros_like(decay)
    for j in range(last_ref.shape[0]):
        gap = (place - 1 - j).astype(f32)
        faded = jnp.exp(-float(length) * jnp.maximum(gap, 0.0) * decay) * last_ref[j]
        carry = carry + jnp.where(gap >= 0.0, faded, jnp.zeros_like(faded))
    for g in range(groups):
        rows = slice(g * BLOCK, (g + 1) * BLOCK)
        fade = jnp.exp(-float(BLOCK) * decay[g : g + 1, :])
        arriving = jnp.where(own, jnp.broadcast_to(carry[g : g + 1, :], (GROUP, BLOCK)), 0.0)
        size = blocks * GROUP
        parts = []
        for b in range(blocks):
            at = g * size + b * GROUP
            parts.append(states_ref[at : at + GROUP, :] + arriving)
            arriving = arriving * fade
        hi, lo = halves(jnp.concatenate(parts, axis=0))
        wide = dot(jnp.concatenate([hi, lo], axis=0), out_hi[rows, :])
        total = wide[:size] + wide[size:] + dot(hi, out_lo[rows, :])
        for b in range(blocks):
            at = b * channels + g * GROUP
            ys[at : at + GROUP, :] = total[b * GROUP : (b + 1) * GROUP]
    for b in range(blocks):
        cols = slice(b * BLOCK, (b + 1) * BLOCK)
        rows = slice(b * channels, (b + 1) * channels)
        result_ref[:, cols] = long_query_ref[:, cols].astype(f32) * (
            ys[rows, :] + within_ref[rows, :]
        )


def sum_over_channels(squares, later):
    both = lax.psum(squares, "core")
    half = squares.shape[0] // 2
    core = lax.axis_index("core")
    mine = lax.dynamic_slice_in_dim(both, core * half, half, 0).astype(bf16)
    count = lax.axis_size("z")
    spread = jnp.broadcast_to(mine[None], (count,) + mine.shape)
    spread, later = lax.optimization_barrier((spread, later))
    gathered = lax.all_to_all(spread, "z", split_axis=0, concat_axis=0, tiled=True)
    own = jnp.sum(gathered.astype(f32), axis=0)
    zero = jnp.zeros_like(own)
    placed = jnp.concatenate(
        [jnp.where(core == 0, own, zero), jnp.where(core == 0, zero, own)]
    )
    return lax.psum(placed, "core"), later


def shape(rows, lanes, dtype=f32):
    return jax.ShapeDtypeStruct((rows, lanes), dtype)


def shards(
    short_query,
    short_key,
    short_value,
    short_taps,
    norm_gain,
    long_key,
    long_query,
    residues,
    decay_rates,
):
    channels, length = short_value.shape
    modes = residues.shape[0]
    groups = channels // GROUP
    blocks = length // BLOCK
    devices = lax.axis_size("ctx")
    rows = blocks * channels
    vmem = pl.BlockSpec(memory_space=pltpu.VMEM)
    hbm = pl.BlockSpec(memory_space=pltpu.HBM)

    short_mix, last = call(
        short_kernel,
        [shape(rows, BLOCK), shape(channels, BLOCK)],
        [hbm] * 3,
        [vmem] * 2,
        [
            pltpu.VMEM((channels, BLOCK), bf16),
            pltpu.VMEM((channels, length), bf16),
            pltpu.VMEM((channels, length), bf16),
            pltpu.VMEM((channels, BLOCK), f32),
            pltpu.VMEM((rows, BLOCK), f32),
            pltpu.VMEM((rows + channels, BLOCK), f32),
            pltpu.SemaphoreType.DMA((2 * PARTS + 1,)),
        ],
        flops=1 << 28,
        bytes_accessed=2 << 20,
        limit=None,
    )(short_taps, short_key, short_value)
    halo = lax.ppermute(last, "ctx", [(i, i + 1) for i in range(devices - 1)])
    mixed, rest, first, query, key = call(
        gate_kernel,
        [shape(rows, BLOCK), shape(blocks, BLOCK)] + [shape(channels, BLOCK)] * 3,
        [vmem] * 2 + [hbm] * 2,
        [vmem] * 5,
        [pltpu.VMEM((channels, length), bf16)] * 2 + [pltpu.SemaphoreType.DMA((2,))],
        flops=1 << 24,
        bytes_accessed=2 << 20,
    )(short_mix, norm_gain.reshape(1, channels), short_query, long_key)
    mixed_first, squares = call(
        join_kernel,
        [shape(channels, BLOCK), shape(blocks, BLOCK)],
        [vmem] * 5,
        [vmem] * 2,
    )(first, halo, query, key, rest)

    total, (residues, decay_rates) = sum_over_channels(squares, (residues, decay_rates))
    weights = residues * jnp.sqrt(-jnp.expm1(-2.0 * decay_rates))

    def columns(value):
        return (
            value.reshape(modes, groups, GROUP).transpose(0, 2, 1).reshape(modes * GROUP, groups)
        )

    decay_cols = columns(decay_rates)
    decay_rows = decay_cols.T
    into_hi, into_lo, out_hi, out_lo, long_taps = call(
        table_kernel,
        [shape(groups * BLOCK, BLOCK, bf16)] * 4 + [shape(channels, BLOCK)],
        [vmem] * 2,
        [vmem] * 5,
        flops=1 << 26,
        bytes_accessed=2 << 20,
    )(decay_cols, columns(weights))
    signal, states, ends = call(
        state_kernel,
        [
            shape(rows, BLOCK),
            shape(rows, BLOCK),
            jax.ShapeDtypeStruct((devices, groups, BLOCK), f32),
        ],
        [vmem] * 6,
        [vmem] * 3,
        bytes_accessed=2 << 20,
        flops=1 << 27,
    )(mixed_first, mixed, total, into_hi, into_lo, decay_rows)
    ends = lax.all_to_all(ends, "ctx", split_axis=0, concat_axis=0, tiled=True)
    within = call(
        within_kernel,
        shape(rows, BLOCK),
        [vmem] * 2,
        vmem,
        bytes_accessed=2 << 20,
        flops=1 << 29,
    )(signal, long_taps)
    place = lax.axis_index("ctx").astype(jnp.int32).reshape(1)
    return call(
        finish_kernel,
        shape(channels, length),
        [pl.BlockSpec(memory_space=pltpu.SMEM)] + [vmem] * 7,
        vmem,
        [pltpu.VMEM((rows, BLOCK), f32)],
        bytes_accessed=2 << 20,
        flops=1 << 27,
    )(place, within, states, ends, out_hi, out_lo, decay_rows, long_query)


def solution(mesh):
    split = Mesh(
        mesh.devices.reshape(mesh.shape["ctx"], mesh.shape["tp"] // 2, 2),
        ("ctx", "z", "core"),
    )
    in_specs = (
        P(TP, "ctx"),
        P(TP, "ctx"),
        P(TP, "ctx"),
        P(TP, None),
        P(TP),
        P(TP, "ctx"),
        P(TP, "ctx"),
        P(None, TP),
        P(None, TP),
    )
    return jax.shard_map(
        shards, mesh=split, in_specs=in_specs, out_specs=P(TP, "ctx"), check_vma=False
    )
```

time: 275 us -> 87.2 us (0.32)
  local copies, waits for them, and re-layouts: 131 us -> 3.48 us
  blocking collectives: 87.1 us -> 18.1 us
  other arithmetic: 24.7 us -> 0.06 us
  waiting for transfers between devices: 4 us -> 27.8 us
  starting transfers between devices: 10.6 us -> 29.4 us
  matrix products: 16 us -> 0 us
  Pallas kernels: 0 us -> 7.81 us
    gather x2 -> x0, local copies, waits for them, and re-layouts: 124 us -> none  [make_band(): jnp.take(filter_taps, jnp.clip(lag_index, 0, tap_count - 1), axis=1)]
    psum x2, blocking collectives: 73.6 us -> 18.1 us  [the longest x1 13.6 us: sum_over_channels(): both = lax.psum(squares, 'core')]
    all_to_all x1 -> x2, waiting for transfers between devices: 4 us -> 27.8 us  [the longest x1 22.9 us: sum_over_channels(): lax.all_to_all(spread, 'z', split_axis=0, concat_axis=0, tiled=True)]
    all_to_all x1 -> x2, starting transfers between devices: 6.7 us -> 25.4 us  [the longest x1 18.1 us: sum_over_channels(): lax.all_to_all(spread, 'z', split_axis=0, concat_axis=0, tiled=True)]
    dot_general x5 -> x0, matrix products: 16 us -> none  [the longest x1 3.78 us: spectral_mix(): jnp.einsum('kcm,mn->kcn', jnp.concatenate([real_prod, imag_prod], axis=2)...]
    all_to_all x1 -> x0, blocking collectives: 13.5 us -> none  [shards(): lax.all_to_all(mixed_whole, 'ctx', split_axis=1, concat_axis=0, tiled=True)]
    reduce_sum x2 -> x1, other arithmetic: 10.6 us -> 0.04 us  [sum_over_channels(): own = jnp.sum(gathered.astype(f32), axis=0)]
    pallas_call x0 -> x7, Pallas kernels: none -> 7.81 us  [the longest x1 3.23 us: shards(): call(short_kernel, [shape(rows, BLOCK), shape(channels, BLOCK)], [hbm] *...]
  transfers between devices with their start and end apart: 2 -> 3, of which waited for: 1 -> 2; matrix products, arithmetic and copies ran while one was open for 53% -> 1% of each run, Pallas kernels for 0% -> 3%
where the time goes in v1:
time: 87.2 us; the launch traced here: 86.8 us
  starting transfers between devices  29.4 us (34%)
  waiting for transfers between devices  27.8 us (32%)
  blocking collectives  18.1 us (21%)
  Pallas kernels  7.81 us (9%)
  local copies, waits for them, and re-layouts  3.48 us (4%)
    all_to_all x1, waiting for transfers between devices, sum_over_channels(): lax.all_to_all(spread, 'z', split_axis=0, concat_axis=0, tiled=True)  22.9 us
    all_to_all x1, starting transfers between devices, sum_over_channels(): lax.all_to_all(spread, 'z', split_axis=0, concat_axis=0, tiled=True)  18.1 us
    psum x1, blocking collectives, sum_over_channels(): both = lax.psum(squares, 'core')  13.6 us
    all_to_all x1, starting transfers between devices, shards(): ends = lax.all_to_all(ends, 'ctx', split_axis=0, concat_axis=0, tiled=True)  7.37 us
    all_to_all x1, waiting for transfers between devices, shards(): ends = lax.all_to_all(ends, 'ctx', split_axis=0, concat_axis=0, tiled=True)  4.88 us
    psum x1, blocking collectives, sum_over_channels(): return (lax.psum(placed, 'core'), later)  4.44 us
    ppermute x1, starting transfers between devices, shards(): halo = lax.ppermute(last, 'ctx', [(i, i + 1) for i in range(devices - 1)])  3.93 us
    pallas_call x1, Pallas kernels, shards(): call(short_kernel, [shape(rows, BLOCK), shape(channels, BLOCK)], [hbm] *...  3.23 us
  transfers between devices with their start and end apart: 3, of which 2 were waited for; matrix products, arithmetic and copies ran while one was open for 1% of the time, Pallas kernels for 3%

profile of v1, /device:TPU:1, one launch (start us, length us, event | category | flops | bytes accessed | tf_op | source)
XLA Modules:
  0.0 86.8 jit_solution(3422968457028194640)
XLA Ops:
  0.0 3.2 %shard_map.91 = (f32[1024,128]{1,0:T(8,128)}, f32[64,128]{1,0:T(8,128)}) custom-call(bf16[64,128]{1,0:T(8,128)(2,1)} %taps_hbm.1, bf16[64,2048]{1,0:T(8,128)(2,1)} %key_hbm.2, bf16[64,2048]{1,0:T(8,128)(2,1)} %value_hbm.1), custom_call_target="tpu_custom_call" | custom-call | flops 268435456 | bytes 2097152 | tf_op jit(solution)/shard_map/pallas_call | solution.py:308
  3.2 3.9 %collective-permute-start = (f32[64,128]{1,0:T(8,128)}, f32[64,128]{1,0:T(8,128)S(1)}, u32[]{:S(2)}, u32[]{:S(2)}) collective-permute-start(f32[64,128]{1,0:T(8,128)} %get-tuple-element.27), channel_id=1, source_target_pairs={{0,64},{64,128},{128,192},{192,256},{256,320},{320,384},{384,448},... | collective-permute-start | bytes 98312 | tf_op jit(solution)/shard_map/ppermute | solution.py:326
  7.2 0.0 copy-start.4
  7.2 0.6 copy-done.4
  7.9 1.0 %copy-done = f32[1024,128]{1,0:T(8,128)S(1)} copy-done((f32[1024,128]{1,0:T(8,128)S(1)}, f32[1024,128]{1,0:T(8,128)}, u32[]{:S(2)}) %copy-start) | copy-done | bytes 524312
  8.9 0.3 shard_map.92
  9.2 13.6 %psum.14 = bf16[16,128]{1,0:T(8,128)(2,1)S(1)} all-reduce(f32[16,128]{1,0:T(8,128)S(1)} %get-tuple-element.33), channel_id=1, replica_groups=mesh['ctx'=16,'z'=32,'core'=2] {'core'}, use_global_device_ids=true, to_apply=%region_0.0 | all-reduce | flops 2048 | bytes 12288 | tf_op jit(solution)/shard_map/psum | solution.py:268
  22.9 0.6 broadcast_in_dim.4
  23.5 18.1 %all-to-all-start = ((bf16[32,8,128]{2,1,0:T(8,128)(2,1)}), bf16[32,8,128]{2,1,0:T(8,128)(2,1)S(1)}, u32[]{:S(2)}, u32[]{:S(2)}) async-start(bf16[32,8,128]{2,1,0:T(8,128)(2,1)} %broadcast_in_dim.4), calls=%async_computation | async-start | bytes 131072 | tf_op jit(solution)/shard_map/all_to_all | solution.py:275
  41.6 0.1 copy.25
  41.7 0.6 copy-done.6
  42.3 0.1 copy.27
  42.4 0.1 copy.28
  42.5 0.1 copy.26
  42.6 0.1 reshape.22
  42.7 0.1 copy.29.decay_ref
  42.8 0.4 shard_map.94
  43.1 22.9 %all-to-all-done = bf16[32,8,128]{2,1,0:T(8,128)(2,1)S(1)} async-done(((bf16[32,8,128]{2,1,0:T(8,128)(2,1)}), bf16[32,8,128]{2,1,0:T(8,128)(2,1)S(1)}, u32[]{:S(2)}, u32[]{:S(2)}) %all-to-all-start) | async-done | bytes 65568 | tf_op jit(solution)/shard_map/all_to_all | solution.py:275
  66.1 4.4 %psum.15.squares_ref = f32[16,128]{1,0:T(8,128)S(1)} all-reduce(f32[16,128]{1,0:T(8,128)S(1)} %pad_maximum_fusion), channel_id=1, replica_groups=mesh['ctx'=16,'z'=32,'core'=2] {'core'}, use_global_device_ids=true, to_apply=%region_2.3 | all-reduce | flops 2048 | bytes 16384 | tf_op jit(solution)/shard_map/psum | solution.py:281
  70.6 1.1 %shard_map.95 = (f32[1024,128]{1,0:T(8,128)S(1)}, f32[1024,128]{1,0:T(8,128)S(1)}, f32[16,8,128]{2,1,0:T(8,128)}) custom-call(f32[64,128]{1,0:T(8,128)S(1)} %get-tuple-element.31.first_ref, f32[1024,128]{1,0:T(8,128)S(1)} %get-tuple-element.32.mixed_ref, f32[16,128]{1,0:T(8,128)S(1)} %psum.15.squares_ref, bf16[1024,128]{1,0:T(8,128)(2,1)S(1)} %get-tuple-element.37.into_hi, ...), custom_call_target="tpu_custom_call" | custom-call | flops 134217728 | bytes 2097152 | tf_op jit(solution)/shard_map/pallas_call | solution.py:361
  71.7 7.4 %all-to-all-start.1 = ((f32[16,8,128]{2,1,0:T(8,128)}), f32[16,8,128]{2,1,0:T(8,128)S(1)}, u32[]{:S(2)}, u32[]{:S(2)}) async-start(f32[16,8,128]{2,1,0:T(8,128)} %get-tuple-element.42), calls=%async_computation.1 | async-start | bytes 131072 | tf_op jit(solution)/shard_map/all_to_all | solution.py:373
  79.1 1.6 %shard_map.96.within_ref = f32[1024,128]{1,0:T(8,128)S(1)} custom-call(f32[1024,128]{1,0:T(8,128)S(1)} %get-tuple-element.39.signal_ref, f32[64,128]{1,0:T(8,128)S(1)} %get-tuple-element.40.taps_ref), custom_call_target="tpu_custom_call" | custom-call | flops 536870912 | bytes 2097152 | tf_op jit(solution)/shard_map/pallas_call | solution.py:374
  80.7 4.9 %all-to-all-done.1.last_ref = f32[16,8,128]{2,1,0:T(8,128)S(1)} async-done(((f32[16,8,128]{2,1,0:T(8,128)}), f32[16,8,128]{2,1,0:T(8,128)S(1)}, u32[]{:S(2)}, u32[]{:S(2)}) %all-to-all-start.1) | async-done | bytes 65568 | tf_op jit(solution)/shard_map/all_to_all | solution.py:373
  85.6 1.2 %shard_map.97 = f32[64,2048]{1,0:T(8,128)} custom-call(s32[1]{0:T(128)} %bitcast.index_ref, f32[1024,128]{1,0:T(8,128)S(1)} %shard_map.96.within_ref, f32[1024,128]{1,0:T(8,128)S(1)} %get-tuple-element.41.states_ref, f32[16,8,128]{2,1,0:T(8,128)S(1)} %all-to-all-done.1.last_ref, bf16[1024,128]{1,0:T(8,128)(2,1)S(1)} %get-tuple-element.43.out_hi, ...), custom_call_target="tpu_custom_call" | custom-call | flops 134217728 | bytes 2097152 | tf_op jit(solution)/shard_map/pallas_call | solution.py:383
  (17 shorter events, 0.1 us)
Async XLA Ops:
  0.0 7.2 %copy-start.2 = (bf16[64,2048]{1,0:T(8,128)(2,1)S(1)}, bf16[64,2048]{1,0:T(8,128)(2,1)}, u32[]{:S(2)}) copy-start(bf16[64,2048]{1,0:T(8,128)(2,1)} %key_hbm.3) | copy-start | bytes 786436
  0.0 7.2 %copy-start.1 = (bf16[64,2048]{1,0:T(8,128)(2,1)S(1)}, bf16[64,2048]{1,0:T(8,128)(2,1)}, u32[]{:S(2)}) copy-start(bf16[64,2048]{1,0:T(8,128)(2,1)} %query_hbm.1) | copy-start | bytes 786436
  3.2 5.9 %collective-permute-start = (f32[64,128]{1,0:T(8,128)}, f32[64,128]{1,0:T(8,128)S(1)}, u32[]{:S(2)}, u32[]{:S(2)}) collective-permute-start(f32[64,128]{1,0:T(8,128)} %get-tuple-element.27), channel_id=1, source_target_pairs={{0,64},{64,128},{128,192},{192,256},{256,320},{320,384},{384,448},... | collective-permute-start | bytes 98312 | tf_op jit(solution)/shard_map/ppermute | solution.py:326
  7.2 0.7 copy-start.4
  7.8 1.0 %copy-start = (f32[1024,128]{1,0:T(8,128)S(1)}, f32[1024,128]{1,0:T(8,128)}, u32[]{:S(2)}) copy-start(f32[1024,128]{1,0:T(8,128)} %get-tuple-element.25.taps_ref) | copy-start | bytes 1572868
  23.5 18.1 %copy-start.5 = (f32[16,64]{1,0:T(8,128)S(1)}, f32[16,64]{1,0:T(8,128)}, u32[]{:S(2)}) copy-start(f32[16,64]{1,0:T(8,128)} %param.17) | copy-start | bytes 12292
  23.5 42.6 %all-to-all-start = ((bf16[32,8,128]{2,1,0:T(8,128)(2,1)}), bf16[32,8,128]{2,1,0:T(8,128)(2,1)S(1)}, u32[]{:S(2)}, u32[]{:S(2)}) async-start(bf16[32,8,128]{2,1,0:T(8,128)(2,1)} %broadcast_in_dim.4), calls=%async_computation | async-start | bytes 131072 | tf_op jit(solution)/shard_map/all_to_all | solution.py:275
  41.6 0.7 copy-start.6
  71.7 13.9 %all-to-all-start.1 = ((f32[16,8,128]{2,1,0:T(8,128)}), f32[16,8,128]{2,1,0:T(8,128)S(1)}, u32[]{:S(2)}, u32[]{:S(2)}) async-start(f32[16,8,128]{2,1,0:T(8,128)} %get-tuple-element.42), calls=%async_computation.1 | async-start | bytes 131072 | tf_op jit(solution)/shard_map/all_to_all | solution.py:373
  79.1 6.5 %copy-start.3 = (bf16[64,2048]{1,0:T(8,128)(2,1)S(1)}, bf16[64,2048]{1,0:T(8,128)(2,1)}, u32[]{:S(2)}) copy-start(bf16[64,2048]{1,0:T(8,128)(2,1)} %long_query_ref.1) | copy-start | bytes 786436

commit v2 on v1

--- a/solution.py
+++ b/solution.py
@@ -272,7 +272,7 @@
     count = lax.axis_size("z")
     spread = jnp.broadcast_to(mine[None], (count,) + mine.shape)
     spread, later = lax.optimization_barrier((spread, later))
-    gathered = lax.all_to_all(spread, "z", split_axis=0, concat_axis=0, tiled=True)
+    gathered = lax.all_to_all(spread, "z", split_axis=0, concat_axis=0, tiled=True, axis_index_groups=[[(i + 16) % 32 for i in range(32)]])
     own = jnp.sum(gathered.astype(f32), axis=0)
     zero = jnp.zeros_like(own)
     placed = jnp.concatenate(

time: 87.2 us -> 74.8 us (0.86)
  waiting for transfers between devices: 27.8 us -> 9.83 us
  starting transfers between devices: 29.4 us -> 36.2 us
  blocking collectives: 18.1 us -> 16.8 us
    all_to_all x1, waiting for transfers between devices: 22.9 us -> 4.94 us  [sum_over_channels(): lax.all_to_all(spread, 'z', split_axis=0, concat_axis=0, tiled=True, axis...]
    all_to_all x1, starting transfers between devices: 18.1 us -> 24.9 us  [sum_over_channels(): lax.all_to_all(spread, 'z', split_axis=0, concat_axis=0, tiled=True, axis...]
    psum x1, blocking collectives: 4.44 us -> 3.17 us  [sum_over_channels(): return (lax.psum(placed, 'core'), later)]
where the time goes in v2:
time: 74.8 us; the launch traced here: 74.4 us
  starting transfers between devices  36.2 us (48%)
  blocking collectives  16.8 us (22%)
  waiting for transfers between devices  9.83 us (13%)
  Pallas kernels  7.82 us (10%)
  local copies, waits for them, and re-layouts  3.48 us (5%)
    all_to_all x1, starting transfers between devices, sum_over_channels(): lax.all_to_all(spread, 'z', split_axis=0, concat_axis=0, tiled=True, axis...  24.9 us
    psum x1, blocking collectives, sum_over_channels(): both = lax.psum(squares, 'core')  13.6 us
    all_to_all x1, starting transfers between devices, shards(): ends = lax.all_to_all(ends, 'ctx', split_axis=0, concat_axis=0, tiled=True)  7.36 us
    all_to_all x1, waiting for transfers between devices, sum_over_channels(): lax.all_to_all(spread, 'z', split_axis=0, concat_axis=0, tiled=True, axis...  4.94 us
    all_to_all x1, waiting for transfers between devices, shards(): ends = lax.all_to_all(ends, 'ctx', split_axis=0, concat_axis=0, tiled=True)  4.88 us
    ppermute x1, starting transfers between devices, shards(): halo = lax.ppermute(last, 'ctx', [(i, i + 1) for i in range(devices - 1)])  3.93 us
    pallas_call x1, Pallas kernels, shards(): call(short_kernel, [shape(rows, BLOCK), shape(channels, BLOCK)], [hbm] *...  3.23 us
    psum x1, blocking collectives, sum_over_channels(): return (lax.psum(placed, 'core'), later)  3.17 us
  transfers between devices with their start and end apart: 3, of which 2 were waited for; matrix products, arithmetic and copies ran while one was open for 1% of the time, Pallas kernels for 3%

profile of v2, /device:TPU:1, one launch (start us, length us, event | category | flops | bytes accessed | tf_op | source)
XLA Modules:
  0.0 74.4 jit_solution(13436125608229898523)
XLA Ops:
  0.0 3.2 %shard_map.91 = (f32[1024,128]{1,0:T(8,128)}, f32[64,128]{1,0:T(8,128)}) custom-call(bf16[64,128]{1,0:T(8,128)(2,1)} %taps_hbm.1, bf16[64,2048]{1,0:T(8,128)(2,1)} %key_hbm.2, bf16[64,2048]{1,0:T(8,128)(2,1)} %value_hbm.1), custom_call_target="tpu_custom_call" | custom-call | flops 268435456 | bytes 2097152 | tf_op jit(solution)/shard_map/pallas_call | solution.py:308
  3.2 3.9 %collective-permute-start = (f32[64,128]{1,0:T(8,128)}, f32[64,128]{1,0:T(8,128)S(1)}, u32[]{:S(2)}, u32[]{:S(2)}) collective-permute-start(f32[64,128]{1,0:T(8,128)} %get-tuple-element.27), channel_id=1, source_target_pairs={{0,64},{64,128},{128,192},{192,256},{256,320},{320,384},{384,448},... | collective-permute-start | bytes 98312 | tf_op jit(solution)/shard_map/ppermute | solution.py:326
  7.2 0.0 copy-start.4
  7.2 0.6 copy-done.4
  7.9 1.0 %copy-done = f32[1024,128]{1,0:T(8,128)S(1)} copy-done((f32[1024,128]{1,0:T(8,128)S(1)}, f32[1024,128]{1,0:T(8,128)}, u32[]{:S(2)}) %copy-start) | copy-done | bytes 524312
  8.9 0.3 shard_map.92
  9.2 13.6 %psum.14 = bf16[16,128]{1,0:T(8,128)(2,1)S(1)} all-reduce(f32[16,128]{1,0:T(8,128)S(1)} %get-tuple-element.33), channel_id=1, replica_groups=mesh['ctx'=16,'z'=32,'core'=2] {'core'}, use_global_device_ids=true, to_apply=%region_0.0 | all-reduce | flops 2048 | bytes 12288 | tf_op jit(solution)/shard_map/psum | solution.py:268
  22.9 0.6 broadcast_in_dim.4
  23.5 24.9 %all-to-all-start = ((bf16[32,8,128]{2,1,0:T(8,128)(2,1)}), bf16[32,8,128]{2,1,0:T(8,128)(2,1)S(1)}, u32[]{:S(2)}, u32[]{:S(2)}) async-start(bf16[32,8,128]{2,1,0:T(8,128)(2,1)} %broadcast_in_dim.4), calls=%async_computation | async-start | bytes 131072 | tf_op jit(solution)/shard_map/all_to_all | solution.py:275
  48.5 0.1 copy.25
  48.6 0.6 copy-done.6
  49.2 0.1 copy.27
  49.3 0.1 copy.28
  49.4 0.1 copy.26
  49.4 0.1 reshape.22
  49.6 0.1 copy.29.decay_ref
  49.7 0.4 shard_map.94
  50.0 4.9 %all-to-all-done = bf16[32,8,128]{2,1,0:T(8,128)(2,1)S(1)} async-done(((bf16[32,8,128]{2,1,0:T(8,128)(2,1)}), bf16[32,8,128]{2,1,0:T(8,128)(2,1)S(1)}, u32[]{:S(2)}, u32[]{:S(2)}) %all-to-all-start) | async-done | bytes 65568 | tf_op jit(solution)/shard_map/all_to_all | solution.py:275
  55.0 3.2 %psum.15.squares_ref = f32[16,128]{1,0:T(8,128)S(1)} all-reduce(f32[16,128]{1,0:T(8,128)S(1)} %pad_maximum_fusion), channel_id=1, replica_groups=mesh['ctx'=16,'z'=32,'core'=2] {'core'}, use_global_device_ids=true, to_apply=%region_2.3 | all-reduce | flops 2048 | bytes 16384 | tf_op jit(solution)/shard_map/psum | solution.py:281
  58.2 1.1 %shard_map.95 = (f32[1024,128]{1,0:T(8,128)S(1)}, f32[1024,128]{1,0:T(8,128)S(1)}, f32[16,8,128]{2,1,0:T(8,128)}) custom-call(f32[64,128]{1,0:T(8,128)S(1)} %get-tuple-element.31.first_ref, f32[1024,128]{1,0:T(8,128)S(1)} %get-tuple-element.32.mixed_ref, f32[16,128]{1,0:T(8,128)S(1)} %psum.15.squares_ref, bf16[1024,128]{1,0:T(8,128)(2,1)S(1)} %get-tuple-element.37.into_hi, ...), custom_call_target="tpu_custom_call" | custom-call | flops 134217728 | bytes 2097152 | tf_op jit(solution)/shard_map/pallas_call | solution.py:361
  59.3 7.4 %all-to-all-start.1 = ((f32[16,8,128]{2,1,0:T(8,128)}), f32[16,8,128]{2,1,0:T(8,128)S(1)}, u32[]{:S(2)}, u32[]{:S(2)}) async-start(f32[16,8,128]{2,1,0:T(8,128)} %get-tuple-element.42), calls=%async_computation.1 | async-start | bytes 131072 | tf_op jit(solution)/shard_map/all_to_all | solution.py:373
  66.7 1.6 %shard_map.96.within_ref = f32[1024,128]{1,0:T(8,128)S(1)} custom-call(f32[1024,128]{1,0:T(8,128)S(1)} %get-tuple-element.39.signal_ref, f32[64,128]{1,0:T(8,128)S(1)} %get-tuple-element.40.taps_ref), custom_call_target="tpu_custom_call" | custom-call | flops 536870912 | bytes 2097152 | tf_op jit(solution)/shard_map/pallas_call | solution.py:374
  68.3 4.9 %all-to-all-done.1.last_ref = f32[16,8,128]{2,1,0:T(8,128)S(1)} async-done(((f32[16,8,128]{2,1,0:T(8,128)}), f32[16,8,128]{2,1,0:T(8,128)S(1)}, u32[]{:S(2)}, u32[]{:S(2)}) %all-to-all-start.1) | async-done | bytes 65568 | tf_op jit(solution)/shard_map/all_to_all | solution.py:373
  73.2 1.2 %shard_map.97 = f32[64,2048]{1,0:T(8,128)} custom-call(s32[1]{0:T(128)} %bitcast.index_ref, f32[1024,128]{1,0:T(8,128)S(1)} %shard_map.96.within_ref, f32[1024,128]{1,0:T(8,128)S(1)} %get-tuple-element.41.states_ref, f32[16,8,128]{2,1,0:T(8,128)S(1)} %all-to-all-done.1.last_ref, bf16[1024,128]{1,0:T(8,128)(2,1)S(1)} %get-tuple-element.43.out_hi, ...), custom_call_target="tpu_custom_call" | custom-call | flops 134217728 | bytes 2097152 | tf_op jit(solution)/shard_map/pallas_call | solution.py:383
  (17 shorter events, 0.1 us)
Async XLA Ops:
  0.0 7.2 %copy-start.2 = (bf16[64,2048]{1,0:T(8,128)(2,1)S(1)}, bf16[64,2048]{1,0:T(8,128)(2,1)}, u32[]{:S(2)}) copy-start(bf16[64,2048]{1,0:T(8,128)(2,1)} %key_hbm.3) | copy-start | bytes 786436
  0.0 7.2 %copy-start.1 = (bf16[64,2048]{1,0:T(8,128)(2,1)S(1)}, bf16[64,2048]{1,0:T(8,128)(2,1)}, u32[]{:S(2)}) copy-start(bf16[64,2048]{1,0:T(8,128)(2,1)} %query_hbm.1) | copy-start | bytes 786436
  3.2 5.9 %collective-permute-start = (f32[64,128]{1,0:T(8,128)}, f32[64,128]{1,0:T(8,128)S(1)}, u32[]{:S(2)}, u32[]{:S(2)}) collective-permute-start(f32[64,128]{1,0:T(8,128)} %get-tuple-element.27), channel_id=1, source_target_pairs={{0,64},{64,128},{128,192},{192,256},{256,320},{320,384},{384,448},... | collective-permute-start | bytes 98312 | tf_op jit(solution)/shard_map/ppermute | solution.py:326
  7.2 0.7 copy-start.4
  7.8 1.0 %copy-start = (f32[1024,128]{1,0:T(8,128)S(1)}, f32[1024,128]{1,0:T(8,128)}, u32[]{:S(2)}) copy-start(f32[1024,128]{1,0:T(8,128)} %get-tuple-element.25.taps_ref) | copy-start | bytes 1572868
  23.5 25.0 %copy-start.5 = (f32[16,64]{1,0:T(8,128)S(1)}, f32[16,64]{1,0:T(8,128)}, u32[]{:S(2)}) copy-start(f32[16,64]{1,0:T(8,128)} %param.17) | copy-start | bytes 12292
  23.5 31.5 %all-to-all-start = ((bf16[32,8,128]{2,1,0:T(8,128)(2,1)}), bf16[32,8,128]{2,1,0:T(8,128)(2,1)S(1)}, u32[]{:S(2)}, u32[]{:S(2)}) async-start(bf16[32,8,128]{2,1,0:T(8,128)(2,1)} %broadcast_in_dim.4), calls=%async_computation | async-start | bytes 131072 | tf_op jit(solution)/shard_map/all_to_all | solution.py:275
  48.5 0.7 copy-start.6
  59.3 13.9 %all-to-all-start.1 = ((f32[16,8,128]{2,1,0:T(8,128)}), f32[16,8,128]{2,1,0:T(8,128)S(1)}, u32[]{:S(2)}, u32[]{:S(2)}) async-start(f32[16,8,128]{2,1,0:T(8,128)} %get-tuple-element.42), calls=%async_computation.1 | async-start | bytes 131072 | tf_op jit(solution)/shard_map/all_to_all | solution.py:373
  66.7 6.5 %copy-start.3 = (bf16[64,2048]{1,0:T(8,128)(2,1)S(1)}, bf16[64,2048]{1,0:T(8,128)(2,1)}, u32[]{:S(2)}) copy-start(bf16[64,2048]{1,0:T(8,128)(2,1)} %long_query_ref.1) | copy-start | bytes 786436

commit v3 on v2

--- a/solution.py
+++ b/solution.py
@@ -113,7 +113,7 @@
                 own, cols
             ].astype(f32)
         lax.fori_loop(i * part, (i + 1) * part, one, 0, unroll=UNROLL)
-    last_ref[...] = ps[blocks * channels :, :]
+    last_ref[...] = ps[blocks * channels :, :].astype(bf16)
     mixed_ref[channels:, :] += ps[channels : blocks * channels, :]
 
 
@@ -164,7 +164,7 @@
 
 
 def join_kernel(short_ref, halo_ref, query_ref, key_ref, rest_ref, mixed_ref, squares_ref):
-    gated = query_ref[...] * (short_ref[...] + halo_ref[...])
+    gated = query_ref[...] * (short_ref[...] + halo_ref[...].astype(f32))
     squares_ref[...] = rest_ref[...]
     squares_ref[0:1, :] = jnp.sum(gated * gated, axis=0, keepdims=True)
     mixed_ref[...] = gated * key_ref[...]
@@ -236,9 +236,11 @@
     place = index_ref[0]
     decay = decay_ref[...]
     carry = jnp.zeros_like(decay)
-    for j in range(last_ref.shape[0]):
+    devices = last_ref.shape[0]
+    for j in range(devices):
         gap = (place - 1 - j).astype(f32)
-        faded = jnp.exp(-float(length) * jnp.maximum(gap, 0.0) * decay) * last_ref[j]
+        slot = (j - devices // 2) % devices
+        faded = jnp.exp(-float(length) * jnp.maximum(gap, 0.0) * decay) * last_ref[slot]
         carry = carry + jnp.where(gap >= 0.0, faded, jnp.zeros_like(faded))
     for g in range(groups):
         rows = slice(g * BLOCK, (g + 1) * BLOCK)
@@ -264,6 +266,14 @@
         )
 
 
+def exchange(spread, axis, first):
+    count = lax.axis_size(axis)
+    group = [(first + i) % count for i in range(count)]
+    return lax.all_to_all(
+        spread, axis, split_axis=0, concat_axis=0, tiled=True, axis_index_groups=[group]
+    )
+
+
 def sum_over_channels(squares, later):
     both = lax.psum(squares, "core")
     half = squares.shape[0] // 2
@@ -272,7 +282,7 @@
     count = lax.axis_size("z")
     spread = jnp.broadcast_to(mine[None], (count,) + mine.shape)
     spread, later = lax.optimization_barrier((spread, later))
-    gathered = lax.all_to_all(spread, "z", split_axis=0, concat_axis=0, tiled=True, axis_index_groups=[[(i + 16) % 32 for i in range(32)]])
+    gathered = exchange(spread, "z", 5 * count // 8)
     own = jnp.sum(gathered.astype(f32), axis=0)
     zero = jnp.zeros_like(own)
     placed = jnp.concatenate(
@@ -307,7 +317,7 @@
 
     short_mix, last = call(
         short_kernel,
-        [shape(rows, BLOCK), shape(channels, BLOCK)],
+        [shape(rows, BLOCK), shape(channels, BLOCK, bf16)],
         [hbm] * 3,
         [vmem] * 2,
         [
@@ -370,7 +380,7 @@
         bytes_accessed=2 << 20,
         flops=1 << 27,
     )(mixed_first, mixed, total, into_hi, into_lo, decay_rows)
-    ends = lax.all_to_all(ends, "ctx", split_axis=0, concat_axis=0, tiled=True)
+    ends = exchange(ends, "ctx", devices // 2)
     within = call(
         within_kernel,
         shape(rows, BLOCK),

time: 74.8 us -> 73.9 us (0.988)
  starting transfers between devices: 36.2 us -> 32.9 us
  waiting for transfers between devices: 9.83 us -> 12.5 us
    all_to_all x2, starting transfers between devices: 32.3 us -> 28.9 us  [exchange(): lax.all_to_all(spread, axis, split_axis=0, concat_axis=0, tiled=True, axi...]
    all_to_all x2, waiting for transfers between devices: 9.83 us -> 12.5 us  [exchange(): lax.all_to_all(spread, axis, split_axis=0, concat_axis=0, tiled=True, axi...]
where the time goes in v3:
time: 73.9 us; the launch traced here: 73.5 us
  starting transfers between devices  32.9 us (45%)
  blocking collectives  16.6 us (22%)
  waiting for transfers between devices  12.5 us (17%)
  Pallas kernels  7.81 us (11%)
  local copies, waits for them, and re-layouts  3.48 us (5%)
    all_to_all x2, starting transfers between devices, exchange(): lax.all_to_all(spread, axis, split_axis=0, concat_axis=0, tiled=True, axi...  28.9 us
    psum x1, blocking collectives, sum_over_channels(): both = lax.psum(squares, 'core')  13.6 us
    all_to_all x2, waiting for transfers between devices, exchange(): lax.all_to_all(spread, axis, split_axis=0, concat_axis=0, tiled=True, axi...  12.5 us
    ppermute x1, starting transfers between devices, shards(): halo = lax.ppermute(last, 'ctx', [(i, i + 1) for i in range(devices - 1)])  3.93 us
    pallas_call x1, Pallas kernels, shards(): call(short_kernel, [shape(rows, BLOCK), shape(channels, BLOCK, bf16)], [h...  3.22 us
    psum x1, blocking collectives, sum_over_channels(): return (lax.psum(placed, 'core'), later)  3 us
    unnamed x14, local copies, waits for them, and re-layouts  2.29 us
    pallas_call x1, Pallas kernels, shards(): call(within_kernel, shape(rows, BLOCK), [vmem] * 2, vmem, bytes_accessed=...  1.61 us
  transfers between devices with their start and end apart: 3, of which 2 were waited for; matrix products, arithmetic and copies ran while one was open for 1% of the time, Pallas kernels for 3%

profile of v3, /device:TPU:1, one launch (start us, length us, event | category | flops | bytes accessed | tf_op | source)
XLA Modules:
  0.0 73.5 jit_solution(4387866932539178496)
XLA Ops:
  0.0 3.2 %shard_map.91 = (f32[1024,128]{1,0:T(8,128)}, bf16[64,128]{1,0:T(8,128)(2,1)}) custom-call(bf16[64,128]{1,0:T(8,128)(2,1)} %taps_hbm.1, bf16[64,2048]{1,0:T(8,128)(2,1)} %key_hbm.2, bf16[64,2048]{1,0:T(8,128)(2,1)} %value_hbm.1), custom_call_target="tpu_custom_call" | custom-call | flops 268435456 | bytes 2097152 | tf_op jit(solution)/shard_map/pallas_call | solution.py:318
  3.2 3.9 %collective-permute-start = (bf16[64,128]{1,0:T(8,128)(2,1)}, bf16[64,128]{1,0:T(8,128)(2,1)S(1)}, u32[]{:S(2)}, u32[]{:S(2)}) collective-permute-start(bf16[64,128]{1,0:T(8,128)(2,1)} %get-tuple-element.27), channel_id=1, source_target_pairs={{0,64},{64,128},{128,192},{192,256},{256,320},{320,384},{384,448},... | collective-permute-start | bytes 49160 | tf_op jit(solution)/shard_map/ppermute | solution.py:336
  7.2 0.0 copy-start.4
  7.2 0.6 copy-done.4
  7.8 1.0 %copy-done = f32[1024,128]{1,0:T(8,128)S(1)} copy-done((f32[1024,128]{1,0:T(8,128)S(1)}, f32[1024,128]{1,0:T(8,128)}, u32[]{:S(2)}) %copy-start) | copy-done | bytes 524312
  8.9 0.3 shard_map.92
  9.2 13.6 %psum.14 = bf16[16,128]{1,0:T(8,128)(2,1)S(1)} all-reduce(f32[16,128]{1,0:T(8,128)S(1)} %get-tuple-element.33), channel_id=1, replica_groups=mesh['ctx'=16,'z'=32,'core'=2] {'core'}, use_global_device_ids=true, to_apply=%region_0.0 | all-reduce | flops 2048 | bytes 12288 | tf_op jit(solution)/shard_map/psum | solution.py:278
  22.8 0.6 broadcast_in_dim.4
  23.5 20.1 %all-to-all-start = ((bf16[32,8,128]{2,1,0:T(8,128)(2,1)}), bf16[32,8,128]{2,1,0:T(8,128)(2,1)S(1)}, u32[]{:S(2)}, u32[]{:S(2)}) async-start(bf16[32,8,128]{2,1,0:T(8,128)(2,1)} %broadcast_in_dim.4), calls=%async_computation | async-start | bytes 131072 | tf_op jit(solution)/shard_map/all_to_all | solution.py:272
  43.7 0.1 copy.25
  43.7 0.6 copy-done.6
  44.4 0.1 copy.27
  44.4 0.1 copy.28
  44.6 0.1 copy.26
  44.6 0.1 reshape.22
  44.7 0.1 copy.29.decay_ref
  44.8 0.4 shard_map.94
  45.2 9.8 %all-to-all-done = bf16[32,8,128]{2,1,0:T(8,128)(2,1)S(1)} async-done(((bf16[32,8,128]{2,1,0:T(8,128)(2,1)}), bf16[32,8,128]{2,1,0:T(8,128)(2,1)S(1)}, u32[]{:S(2)}, u32[]{:S(2)}) %all-to-all-start) | async-done | bytes 65568 | tf_op jit(solution)/shard_map/all_to_all | solution.py:272
  55.1 3.0 %psum.15.squares_ref = f32[16,128]{1,0:T(8,128)S(1)} all-reduce(f32[16,128]{1,0:T(8,128)S(1)} %pad_maximum_fusion), channel_id=1, replica_groups=mesh['ctx'=16,'z'=32,'core'=2] {'core'}, use_global_device_ids=true, to_apply=%region_2.3 | all-reduce | flops 2048 | bytes 16384 | tf_op jit(solution)/shard_map/psum | solution.py:291
  58.1 1.1 %shard_map.95 = (f32[1024,128]{1,0:T(8,128)S(1)}, f32[1024,128]{1,0:T(8,128)S(1)}, f32[16,8,128]{2,1,0:T(8,128)}) custom-call(f32[64,128]{1,0:T(8,128)S(1)} %get-tuple-element.31.first_ref, f32[1024,128]{1,0:T(8,128)S(1)} %get-tuple-element.32.mixed_ref, f32[16,128]{1,0:T(8,128)S(1)} %psum.15.squares_ref, bf16[1024,128]{1,0:T(8,128)(2,1)S(1)} %get-tuple-element.37.into_hi, ...), custom_call_target="tpu_custom_call" | custom-call | flops 134217728 | bytes 2097152 | tf_op jit(solution)/shard_map/pallas_call | solution.py:371
  59.2 8.8 %all-to-all-start.1 = ((f32[16,8,128]{2,1,0:T(8,128)}), f32[16,8,128]{2,1,0:T(8,128)S(1)}, u32[]{:S(2)}, u32[]{:S(2)}) async-start(f32[16,8,128]{2,1,0:T(8,128)} %get-tuple-element.42), calls=%async_computation.1 | async-start | bytes 131072 | tf_op jit(solution)/shard_map/all_to_all | solution.py:272
  68.0 1.6 %shard_map.96.within_ref = f32[1024,128]{1,0:T(8,128)S(1)} custom-call(f32[1024,128]{1,0:T(8,128)S(1)} %get-tuple-element.39.signal_ref, f32[64,128]{1,0:T(8,128)S(1)} %get-tuple-element.40.taps_ref), custom_call_target="tpu_custom_call" | custom-call | flops 536870912 | bytes 2097152 | tf_op jit(solution)/shard_map/pallas_call | solution.py:384
  69.7 2.7 %all-to-all-done.1.last_ref = f32[16,8,128]{2,1,0:T(8,128)S(1)} async-done(((f32[16,8,128]{2,1,0:T(8,128)}), f32[16,8,128]{2,1,0:T(8,128)S(1)}, u32[]{:S(2)}, u32[]{:S(2)}) %all-to-all-start.1) | async-done | bytes 65568 | tf_op jit(solution)/shard_map/all_to_all | solution.py:272
  72.3 1.2 %shard_map.97 = f32[64,2048]{1,0:T(8,128)} custom-call(s32[1]{0:T(128)} %bitcast.index_ref, f32[1024,128]{1,0:T(8,128)S(1)} %shard_map.96.within_ref, f32[1024,128]{1,0:T(8,128)S(1)} %get-tuple-element.41.states_ref, f32[16,8,128]{2,1,0:T(8,128)S(1)} %all-to-all-done.1.last_ref, bf16[1024,128]{1,0:T(8,128)(2,1)S(1)} %get-tuple-element.43.out_hi, ...), custom_call_target="tpu_custom_call" | custom-call | flops 134217728 | bytes 2097152 | tf_op jit(solution)/shard_map/pallas_call | solution.py:393
  (17 shorter events, 0.1 us)
Async XLA Ops:
  0.0 7.2 %copy-start.2 = (bf16[64,2048]{1,0:T(8,128)(2,1)S(1)}, bf16[64,2048]{1,0:T(8,128)(2,1)}, u32[]{:S(2)}) copy-start(bf16[64,2048]{1,0:T(8,128)(2,1)} %key_hbm.3) | copy-start | bytes 786436
  0.0 7.2 %copy-start.1 = (bf16[64,2048]{1,0:T(8,128)(2,1)S(1)}, bf16[64,2048]{1,0:T(8,128)(2,1)}, u32[]{:S(2)}) copy-start(bf16[64,2048]{1,0:T(8,128)(2,1)} %query_hbm.1) | copy-start | bytes 786436
  3.2 5.9 %collective-permute-start = (bf16[64,128]{1,0:T(8,128)(2,1)}, bf16[64,128]{1,0:T(8,128)(2,1)S(1)}, u32[]{:S(2)}, u32[]{:S(2)}) collective-permute-start(bf16[64,128]{1,0:T(8,128)(2,1)} %get-tuple-element.27), channel_id=1, source_target_pairs={{0,64},{64,128},{128,192},{192,256},{256,320},{320,384},{384,448},... | collective-permute-start | bytes 49160 | tf_op jit(solution)/shard_map/ppermute | solution.py:336
  7.2 0.7 copy-start.4
  7.8 1.0 %copy-start = (f32[1024,128]{1,0:T(8,128)S(1)}, f32[1024,128]{1,0:T(8,128)}, u32[]{:S(2)}) copy-start(f32[1024,128]{1,0:T(8,128)} %get-tuple-element.25.taps_ref) | copy-start | bytes 1572868
  23.5 20.2 %copy-start.5 = (f32[16,64]{1,0:T(8,128)S(1)}, f32[16,64]{1,0:T(8,128)}, u32[]{:S(2)}) copy-start(f32[16,64]{1,0:T(8,128)} %param.17) | copy-start | bytes 12292
  23.5 31.6 %all-to-all-start = ((bf16[32,8,128]{2,1,0:T(8,128)(2,1)}), bf16[32,8,128]{2,1,0:T(8,128)(2,1)S(1)}, u32[]{:S(2)}, u32[]{:S(2)}) async-start(bf16[32,8,128]{2,1,0:T(8,128)(2,1)} %broadcast_in_dim.4), calls=%async_computation | async-start | bytes 131072 | tf_op jit(solution)/shard_map/all_to_all | solution.py:272
  43.6 0.7 copy-start.6
  59.2 13.1 %all-to-all-start.1 = ((f32[16,8,128]{2,1,0:T(8,128)}), f32[16,8,128]{2,1,0:T(8,128)S(1)}, u32[]{:S(2)}, u32[]{:S(2)}) async-start(f32[16,8,128]{2,1,0:T(8,128)} %get-tuple-element.42), calls=%async_computation.1 | async-start | bytes 131072 | tf_op jit(solution)/shard_map/all_to_all | solution.py:272
  68.0 4.3 %copy-start.3 = (bf16[64,2048]{1,0:T(8,128)(2,1)S(1)}, bf16[64,2048]{1,0:T(8,128)(2,1)}, u32[]{:S(2)}) copy-start(bf16[64,2048]{1,0:T(8,128)(2,1)} %long_query_ref.1) | copy-start | bytes 786436

commit v4 on v3

--- a/solution.py
+++ b/solution.py
@@ -88,6 +88,7 @@
             copy.start()
         copies.append(pair)
     upper = upper_mask()
+    opening = lax.broadcasted_iota(jnp.int32, (blocks, BLOCK), 0) == 0
 
     def one(c, carry):
         ring = circulant(taps[pl.ds(c, 1), :])
@@ -96,8 +97,11 @@
             [jnp.where(upper, ring, zero), jnp.where(upper, zero, ring)], axis=1
         ).astype(bf16)
         both = dot(xs[pl.ds(c, blocks, stride=channels), :].astype(bf16), band)
-        mixed_ref[pl.ds(c, blocks, stride=channels), :] = both[:, :BLOCK]
-        ps[pl.ds(c + channels, blocks, stride=channels), :] = both[:, BLOCK:]
+        behind = pltpu.roll(both[:, BLOCK:], 1, 0)
+        mixed_ref[pl.ds(c * blocks, blocks), :] = both[:, :BLOCK] + jnp.where(
+            opening, zero[:blocks], behind
+        )
+        ps[pl.ds(c, 1), :] = behind[:1]
         return carry
 
     first.wait()
@@ -113,8 +117,7 @@
                 own, cols
             ].astype(f32)
         lax.fori_loop(i * part, (i + 1) * part, one, 0, unroll=UNROLL)
-    last_ref[...] = ps[blocks * channels :, :].astype(bf16)
-    mixed_ref[channels:, :] += ps[channels : blocks * channels, :]
+    last_ref[...] = ps[...].astype(bf16)
 
 
 def gate_kernel(
@@ -137,13 +140,15 @@
         copy.wait()
     open_query[...] = query_ref[:, :BLOCK].astype(f32)
     open_key[...] = gain * key_ref[:, :BLOCK].astype(f32)
-    open_mix[...] = taps_ref[:channels, :]
+    open_mix[...] = taps_ref[pl.ds(0, channels, stride=blocks), :]
     mixed_ref[:channels, :] = jnp.zeros((channels, BLOCK), f32)
     squares_ref[0:1, :] = jnp.zeros((1, BLOCK), f32)
     for b in range(1, blocks):
         cols = slice(b * BLOCK, (b + 1) * BLOCK)
         rows = slice(b * channels, (b + 1) * channels)
-        gated = query_ref[:, cols].astype(f32) * taps_ref[rows, :]
+        gated = query_ref[:, cols].astype(f32) * taps_ref[
+            pl.ds(b, channels, stride=blocks), :
+        ]
         squares_ref[b : b + 1, :] = jnp.sum(gated * gated, axis=0, keepdims=True)
         mixed_ref[rows, :] = gated * gain * key_ref[:, cols].astype(f32)
 
@@ -226,7 +231,7 @@
 
 def finish_kernel(
     index_ref, within_ref, states_ref, last_ref, out_hi, out_lo, decay_ref,
-    long_query_ref, result_ref, ys,
+    long_query_ref, result_hbm, result_ref, sems,
 ):
     groups = decay_ref.shape[0]
     channels = groups * GROUP
@@ -242,6 +247,7 @@
         slot = (j - devices // 2) % devices
         faded = jnp.exp(-float(length) * jnp.maximum(gap, 0.0) * decay) * last_ref[slot]
         carry = carry + jnp.where(gap >= 0.0, faded, jnp.zeros_like(faded))
+    sends = []
     for g in range(groups):
         rows = slice(g * BLOCK, (g + 1) * BLOCK)
         fade = jnp.exp(-float(BLOCK) * decay[g : g + 1, :])
@@ -255,15 +261,22 @@
         hi, lo = halves(jnp.concatenate(parts, axis=0))
         wide = dot(jnp.concatenate([hi, lo], axis=0), out_hi[rows, :])
         total = wide[:size] + wide[size:] + dot(hi, out_lo[rows, :])
+        strip = slice(g * GROUP, (g + 1) * GROUP)
         for b in range(blocks):
             at = b * channels + g * GROUP
-            ys[at : at + GROUP, :] = total[b * GROUP : (b + 1) * GROUP]
-    for b in range(blocks):
-        cols = slice(b * BLOCK, (b + 1) * BLOCK)
-        rows = slice(b * channels, (b + 1) * channels)
-        result_ref[:, cols] = long_query_ref[:, cols].astype(f32) * (
-            ys[rows, :] + within_ref[rows, :]
+            cols = slice(b * BLOCK, (b + 1) * BLOCK)
+            result_ref[strip, cols] = long_query_ref[strip, cols].astype(f32) * (
+                total[b * GROUP : (b + 1) * GROUP] + within_ref[at : at + GROUP, :]
+            )
+        send = pltpu.make_async_copy(
+            result_ref.at[pl.ds(g * GROUP, GROUP)],
+            result_hbm.at[pl.ds(g * GROUP, GROUP)],
+            sems.at[g],
         )
+        send.start()
+        sends.append(send)
+    for send in sends:
+        send.wait()
 
 
 def exchange(spread, axis, first):
@@ -326,7 +339,7 @@
             pltpu.VMEM((channels, length), bf16),
             pltpu.VMEM((channels, BLOCK), f32),
             pltpu.VMEM((rows, BLOCK), f32),
-            pltpu.VMEM((rows + channels, BLOCK), f32),
+            pltpu.VMEM((channels, BLOCK), f32),
             pltpu.SemaphoreType.DMA((2 * PARTS + 1,)),
         ],
         flops=1 << 28,
@@ -394,8 +407,8 @@
         finish_kernel,
         shape(channels, length),
         [pl.BlockSpec(memory_space=pltpu.SMEM)] + [vmem] * 7,
-        vmem,
-        [pltpu.VMEM((rows, BLOCK), f32)],
+        hbm,
+        [pltpu.VMEM((channels, length), f32), pltpu.SemaphoreType.DMA((groups,))],
         bytes_accessed=2 << 20,
         flops=1 << 27,
     )(place, within, states, ends, out_hi, out_lo, decay_rows, long_query)

time: 73.9 us -> 73.5 us (level)
  no operation moved by 1% of the time
where the time goes in v4:
time: 73.5 us; the launch traced here: 73 us
  starting transfers between devices  32.7 us (44%)
  blocking collectives  16.6 us (23%)
  waiting for transfers between devices  12.5 us (17%)
  Pallas kernels  7.49 us (10%)
  local copies, waits for them, and re-layouts  3.48 us (5%)
    all_to_all x2, starting transfers between devices, exchange(): lax.all_to_all(spread, axis, split_axis=0, concat_axis=0, tiled=True, axi...  28.8 us
    psum x1, blocking collectives, sum_over_channels(): both = lax.psum(squares, 'core')  13.6 us
    all_to_all x2, waiting for transfers between devices, exchange(): lax.all_to_all(spread, axis, split_axis=0, concat_axis=0, tiled=True, axi...  12.5 us
    ppermute x1, starting transfers between devices, shards(): halo = lax.ppermute(last, 'ctx', [(i, i + 1) for i in range(devices - 1)])  3.93 us
    psum x1, blocking collectives, sum_over_channels(): return (lax.psum(placed, 'core'), later)  3 us
    pallas_call x1, Pallas kernels, shards(): call(short_kernel, [shape(rows, BLOCK), shape(channels, BLOCK, bf16)], [h...  2.83 us
    unnamed x14, local copies, waits for them, and re-layouts  2.29 us
    pallas_call x1, Pallas kernels, shards(): call(within_kernel, shape(rows, BLOCK), [vmem] * 2, vmem, bytes_accessed=...  1.61 us
  transfers between devices with their start and end apart: 3, of which 2 were waited for; matrix products, arithmetic and copies ran while one was open for 1% of the time, Pallas kernels for 3%

profile of v4, /device:TPU:1, one launch (start us, length us, event | category | flops | bytes accessed | tf_op | source)
XLA Modules:
  0.0 73.0 jit_solution(9012547381032439620)
XLA Ops:
  0.0 2.8 %shard_map.91 = (f32[1024,128]{1,0:T(8,128)}, bf16[64,128]{1,0:T(8,128)(2,1)}) custom-call(bf16[64,128]{1,0:T(8,128)(2,1)} %taps_hbm.1, bf16[64,2048]{1,0:T(8,128)(2,1)} %key_hbm.2, bf16[64,2048]{1,0:T(8,128)(2,1)} %value_hbm.1), custom_call_target="tpu_custom_call" | custom-call | flops 268435456 | bytes 2097152 | tf_op jit(solution)/shard_map/pallas_call | solution.py:331
  2.8 3.9 %collective-permute-start = (bf16[64,128]{1,0:T(8,128)(2,1)}, bf16[64,128]{1,0:T(8,128)(2,1)S(1)}, u32[]{:S(2)}, u32[]{:S(2)}) collective-permute-start(bf16[64,128]{1,0:T(8,128)(2,1)} %get-tuple-element.27), channel_id=1, source_target_pairs={{0,64},{64,128},{128,192},{192,256},{256,320},{320,384},{384,448},... | collective-permute-start | bytes 49160 | tf_op jit(solution)/shard_map/ppermute | solution.py:349
  6.8 0.6 copy-done.4
  7.5 1.0 %copy-done = f32[1024,128]{1,0:T(8,128)S(1)} copy-done((f32[1024,128]{1,0:T(8,128)S(1)}, f32[1024,128]{1,0:T(8,128)}, u32[]{:S(2)}) %copy-start) | copy-done | bytes 524312
  8.5 0.4 shard_map.92
  9.0 13.6 %psum.14 = bf16[16,128]{1,0:T(8,128)(2,1)S(1)} all-reduce(f32[16,128]{1,0:T(8,128)S(1)} %get-tuple-element.33), channel_id=1, replica_groups=mesh['ctx'=16,'z'=32,'core'=2] {'core'}, use_global_device_ids=true, to_apply=%region_0.0 | all-reduce | flops 2048 | bytes 12288 | tf_op jit(solution)/shard_map/psum | solution.py:291
  22.6 0.6 broadcast_in_dim.4
  23.2 20.1 %all-to-all-start = ((bf16[32,8,128]{2,1,0:T(8,128)(2,1)}), bf16[32,8,128]{2,1,0:T(8,128)(2,1)S(1)}, u32[]{:S(2)}, u32[]{:S(2)}) async-start(bf16[32,8,128]{2,1,0:T(8,128)(2,1)} %broadcast_in_dim.4), calls=%async_computation | async-start | bytes 131072 | tf_op jit(solution)/shard_map/all_to_all | solution.py:285
  43.4 0.0 copy-start.6
  43.4 0.1 copy.25
  43.5 0.6 copy-done.6
  44.1 0.1 copy.27
  44.2 0.1 copy.28
  44.3 0.1 copy.26
  44.4 0.1 reshape.22
  44.5 0.1 copy.29.decay_ref
  44.6 0.4 shard_map.94
  45.0 9.8 %all-to-all-done = bf16[32,8,128]{2,1,0:T(8,128)(2,1)S(1)} async-done(((bf16[32,8,128]{2,1,0:T(8,128)(2,1)}), bf16[32,8,128]{2,1,0:T(8,128)(2,1)S(1)}, u32[]{:S(2)}, u32[]{:S(2)}) %all-to-all-start) | async-done | bytes 65568 | tf_op jit(solution)/shard_map/all_to_all | solution.py:285
  54.9 3.0 %psum.15.squares_ref = f32[16,128]{1,0:T(8,128)S(1)} all-reduce(f32[16,128]{1,0:T(8,128)S(1)} %pad_maximum_fusion), channel_id=1, replica_groups=mesh['ctx'=16,'z'=32,'core'=2] {'core'}, use_global_device_ids=true, to_apply=%region_2.3 | all-reduce | flops 2048 | bytes 16384 | tf_op jit(solution)/shard_map/psum | solution.py:304
  57.9 1.1 %shard_map.95 = (f32[1024,128]{1,0:T(8,128)S(1)}, f32[1024,128]{1,0:T(8,128)S(1)}, f32[16,8,128]{2,1,0:T(8,128)}) custom-call(f32[64,128]{1,0:T(8,128)S(1)} %get-tuple-element.31.first_ref, f32[1024,128]{1,0:T(8,128)S(1)} %get-tuple-element.32.mixed_ref, f32[16,128]{1,0:T(8,128)S(1)} %psum.15.squares_ref, bf16[1024,128]{1,0:T(8,128)(2,1)S(1)} %get-tuple-element.37.into_hi, ...), custom_call_target="tpu_custom_call" | custom-call | flops 134217728 | bytes 2097152 | tf_op jit(solution)/shard_map/pallas_call | solution.py:384
  59.0 8.7 %all-to-all-start.1 = ((f32[16,8,128]{2,1,0:T(8,128)}), f32[16,8,128]{2,1,0:T(8,128)S(1)}, u32[]{:S(2)}, u32[]{:S(2)}) async-start(f32[16,8,128]{2,1,0:T(8,128)} %get-tuple-element.42), calls=%async_computation.1 | async-start | bytes 131072 | tf_op jit(solution)/shard_map/all_to_all | solution.py:285
  67.7 1.6 %shard_map.96.within_ref = f32[1024,128]{1,0:T(8,128)S(1)} custom-call(f32[1024,128]{1,0:T(8,128)S(1)} %get-tuple-element.39.signal_ref, f32[64,128]{1,0:T(8,128)S(1)} %get-tuple-element.40.taps_ref), custom_call_target="tpu_custom_call" | custom-call | flops 536870912 | bytes 2097152 | tf_op jit(solution)/shard_map/pallas_call | solution.py:397
  69.3 2.7 %all-to-all-done.1.last_ref = f32[16,8,128]{2,1,0:T(8,128)S(1)} async-done(((f32[16,8,128]{2,1,0:T(8,128)}), f32[16,8,128]{2,1,0:T(8,128)S(1)}, u32[]{:S(2)}, u32[]{:S(2)}) %all-to-all-start.1) | async-done | bytes 65568 | tf_op jit(solution)/shard_map/all_to_all | solution.py:285
  71.9 1.1 %shard_map.97 = f32[64,2048]{1,0:T(8,128)} custom-call(s32[1]{0:T(128)} %bitcast.index_ref, f32[1024,128]{1,0:T(8,128)S(1)} %shard_map.96.within_ref, f32[1024,128]{1,0:T(8,128)S(1)} %get-tuple-element.41.states_ref, f32[16,8,128]{2,1,0:T(8,128)S(1)} %all-to-all-done.1.last_ref, bf16[1024,128]{1,0:T(8,128)(2,1)S(1)} %get-tuple-element.43.out_hi, ...), custom_call_target="tpu_custom_call" | custom-call | flops 134217728 | bytes 2097152 | tf_op jit(solution)/shard_map/pallas_call | solution.py:406
  (17 shorter events, 0.1 us)
Async XLA Ops:
  0.0 6.8 %copy-start.2 = (bf16[64,2048]{1,0:T(8,128)(2,1)S(1)}, bf16[64,2048]{1,0:T(8,128)(2,1)}, u32[]{:S(2)}) copy-start(bf16[64,2048]{1,0:T(8,128)(2,1)} %key_hbm.3) | copy-start | bytes 786436
  0.0 6.8 %copy-start.1 = (bf16[64,2048]{1,0:T(8,128)(2,1)S(1)}, bf16[64,2048]{1,0:T(8,128)(2,1)}, u32[]{:S(2)}) copy-start(bf16[64,2048]{1,0:T(8,128)(2,1)} %query_hbm.1) | copy-start | bytes 786436
  2.8 6.1 %collective-permute-start = (bf16[64,128]{1,0:T(8,128)(2,1)}, bf16[64,128]{1,0:T(8,128)(2,1)S(1)}, u32[]{:S(2)}, u32[]{:S(2)}) collective-permute-start(bf16[64,128]{1,0:T(8,128)(2,1)} %get-tuple-element.27), channel_id=1, source_target_pairs={{0,64},{64,128},{128,192},{192,256},{256,320},{320,384},{384,448},... | collective-permute-start | bytes 49160 | tf_op jit(solution)/shard_map/ppermute | solution.py:349
  6.8 0.7 copy-start.4
  7.5 1.0 %copy-start = (f32[1024,128]{1,0:T(8,128)S(1)}, f32[1024,128]{1,0:T(8,128)}, u32[]{:S(2)}) copy-start(f32[1024,128]{1,0:T(8,128)} %get-tuple-element.25.taps_ref) | copy-start | bytes 1572868
  23.2 20.2 %copy-start.5 = (f32[16,64]{1,0:T(8,128)S(1)}, f32[16,64]{1,0:T(8,128)}, u32[]{:S(2)}) copy-start(f32[16,64]{1,0:T(8,128)} %param.17) | copy-start | bytes 12292
  23.2 31.6 %all-to-all-start = ((bf16[32,8,128]{2,1,0:T(8,128)(2,1)}), bf16[32,8,128]{2,1,0:T(8,128)(2,1)S(1)}, u32[]{:S(2)}, u32[]{:S(2)}) async-start(bf16[32,8,128]{2,1,0:T(8,128)(2,1)} %broadcast_in_dim.4), calls=%async_computation | async-start | bytes 131072 | tf_op jit(solution)/shard_map/all_to_all | solution.py:285
  43.4 0.7 copy-start.6
  59.0 12.9 %all-to-all-start.1 = ((f32[16,8,128]{2,1,0:T(8,128)}), f32[16,8,128]{2,1,0:T(8,128)S(1)}, u32[]{:S(2)}, u32[]{:S(2)}) async-start(f32[16,8,128]{2,1,0:T(8,128)} %get-tuple-element.42), calls=%async_computation.1 | async-start | bytes 131072 | tf_op jit(solution)/shard_map/all_to_all | solution.py:285
  67.7 4.3 %copy-start.3 = (bf16[64,2048]{1,0:T(8,128)(2,1)S(1)}, bf16[64,2048]{1,0:T(8,128)(2,1)}, u32[]{:S(2)}) copy-start(bf16[64,2048]{1,0:T(8,128)(2,1)} %long_query_ref.1) | copy-start | bytes 786436

commit v5 on v4

--- a/solution.py
+++ b/solution.py
@@ -279,9 +279,7 @@
         send.wait()
 
 
-def exchange(spread, axis, first):
-    count = lax.axis_size(axis)
-    group = [(first + i) % count for i in range(count)]
+def exchange(spread, axis, group):
     return lax.all_to_all(
         spread, axis, split_axis=0, concat_axis=0, tiled=True, axis_index_groups=[group]
     )
@@ -295,7 +293,9 @@
     count = lax.axis_size("z")
     spread = jnp.broadcast_to(mine[None], (count,) + mine.shape)
     spread, later = lax.optimization_barrier((spread, later))
-    gathered = exchange(spread, "z", 5 * count // 8)
+    meet, near = 5 * count // 8, count // 8
+    group = [meet, *range(near), *range(meet + 1, count), *range(near, meet)]
+    gathered = exchange(spread, "z", group)
     own = jnp.sum(gathered.astype(f32), axis=0)
     zero = jnp.zeros_like(own)
     placed = jnp.concatenate(
@@ -393,7 +393,9 @@
         bytes_accessed=2 << 20,
         flops=1 << 27,
     )(mixed_first, mixed, total, into_hi, into_lo, decay_rows)
-    ends = exchange(ends, "ctx", devices // 2)
+    ends = exchange(
+        ends, "ctx", [(devices // 2 + i) % devices for i in range(devices)]
+    )
     within = call(
         within_kernel,
         shape(rows, BLOCK),

time: 73.5 us -> 73.7 us (level)
  no operation moved by 1% of the time
where the time goes in v5:
time: 73.7 us; the launch traced here: 73.2 us
  starting transfers between devices  32.7 us (44%)
  blocking collectives  17.2 us (23%)
  waiting for transfers between devices  12.1 us (16%)
  Pallas kernels  7.49 us (10%)
  local copies, waits for them, and re-layouts  3.48 us (5%)
    all_to_all x2, starting transfers between devices, exchange(): lax.all_to_all(spread, axis, split_axis=0, concat_axis=0, tiled=True, axi...  28.8 us
    psum x1, blocking collectives, sum_over_channels(): both = lax.psum(squares, 'core')  13.6 us
    all_to_all x2, waiting for transfers between devices, exchange(): lax.all_to_all(spread, axis, split_axis=0, concat_axis=0, tiled=True, axi...  12.1 us
    ppermute x1, starting transfers between devices, shards(): halo = lax.ppermute(last, 'ctx', [(i, i + 1) for i in range(devices - 1)])  3.93 us
    psum x1, blocking collectives, sum_over_channels(): return (lax.psum(placed, 'core'), later)  3.56 us
    pallas_call x1, Pallas kernels, shards(): call(short_kernel, [shape(rows, BLOCK), shape(channels, BLOCK, bf16)], [h...  2.83 us
    unnamed x14, local copies, waits for them, and re-layouts  2.29 us
    pallas_call x1, Pallas kernels, shards(): call(within_kernel, shape(rows, BLOCK), [vmem] * 2, vmem, bytes_accessed=...  1.61 us
  transfers between devices with their start and end apart: 3, of which 2 were waited for; matrix products, arithmetic and copies ran while one was open for 1% of the time, Pallas kernels for 3%

profile of v5, /device:TPU:1, one launch (start us, length us, event | category | flops | bytes accessed | tf_op | source)
XLA Modules:
  0.0 73.2 jit_solution(17178735821986861536)
XLA Ops:
  0.0 2.8 %shard_map.91 = (f32[1024,128]{1,0:T(8,128)}, bf16[64,128]{1,0:T(8,128)(2,1)}) custom-call(bf16[64,128]{1,0:T(8,128)(2,1)} %taps_hbm.1, bf16[64,2048]{1,0:T(8,128)(2,1)} %key_hbm.2, bf16[64,2048]{1,0:T(8,128)(2,1)} %value_hbm.1), custom_call_target="tpu_custom_call" | custom-call | flops 268435456 | bytes 2097152 | tf_op jit(solution)/shard_map/pallas_call | solution.py:331
  2.8 3.9 %collective-permute-start = (bf16[64,128]{1,0:T(8,128)(2,1)}, bf16[64,128]{1,0:T(8,128)(2,1)S(1)}, u32[]{:S(2)}, u32[]{:S(2)}) collective-permute-start(bf16[64,128]{1,0:T(8,128)(2,1)} %get-tuple-element.27), channel_id=1, source_target_pairs={{0,64},{64,128},{128,192},{192,256},{256,320},{320,384},{384,448},... | collective-permute-start | bytes 49160 | tf_op jit(solution)/shard_map/ppermute | solution.py:349
  6.8 0.0 copy-start.4
  6.8 0.6 copy-done.4
  7.5 1.0 %copy-done = f32[1024,128]{1,0:T(8,128)S(1)} copy-done((f32[1024,128]{1,0:T(8,128)S(1)}, f32[1024,128]{1,0:T(8,128)}, u32[]{:S(2)}) %copy-start) | copy-done | bytes 524312
  8.5 0.4 shard_map.92
  9.0 13.6 %psum.14 = bf16[16,128]{1,0:T(8,128)(2,1)S(1)} all-reduce(f32[16,128]{1,0:T(8,128)S(1)} %get-tuple-element.33), channel_id=1, replica_groups=mesh['ctx'=16,'z'=32,'core'=2] {'core'}, use_global_device_ids=true, to_apply=%region_0.0 | all-reduce | flops 2048 | bytes 12288 | tf_op jit(solution)/shard_map/psum | solution.py:289
  22.6 0.6 broadcast_in_dim.4
  23.2 20.1 %all-to-all-start = ((bf16[32,8,128]{2,1,0:T(8,128)(2,1)}), bf16[32,8,128]{2,1,0:T(8,128)(2,1)S(1)}, u32[]{:S(2)}, u32[]{:S(2)}) async-start(bf16[32,8,128]{2,1,0:T(8,128)(2,1)} %broadcast_in_dim.4), calls=%async_computation | async-start | bytes 131072 | tf_op jit(solution)/shard_map/all_to_all | solution.py:283
  43.4 0.1 copy.25
  43.5 0.6 copy-done.6
  44.1 0.1 copy.27
  44.2 0.1 copy.28
  44.3 0.1 copy.26
  44.4 0.1 reshape.22
  44.5 0.1 copy.29.decay_ref
  44.6 0.4 shard_map.94
  44.9 9.5 %all-to-all-done = bf16[32,8,128]{2,1,0:T(8,128)(2,1)S(1)} async-done(((bf16[32,8,128]{2,1,0:T(8,128)(2,1)}), bf16[32,8,128]{2,1,0:T(8,128)(2,1)S(1)}, u32[]{:S(2)}, u32[]{:S(2)}) %all-to-all-start) | async-done | bytes 65568 | tf_op jit(solution)/shard_map/all_to_all | solution.py:283
  54.5 3.6 %psum.15.squares_ref = f32[16,128]{1,0:T(8,128)S(1)} all-reduce(f32[16,128]{1,0:T(8,128)S(1)} %pad_maximum_fusion), channel_id=1, replica_groups=mesh['ctx'=16,'z'=32,'core'=2] {'core'}, use_global_device_ids=true, to_apply=%region_2.3 | all-reduce | flops 2048 | bytes 16384 | tf_op jit(solution)/shard_map/psum | solution.py:304
  58.0 1.1 %shard_map.95 = (f32[1024,128]{1,0:T(8,128)S(1)}, f32[1024,128]{1,0:T(8,128)S(1)}, f32[16,8,128]{2,1,0:T(8,128)}) custom-call(f32[64,128]{1,0:T(8,128)S(1)} %get-tuple-element.31.first_ref, f32[1024,128]{1,0:T(8,128)S(1)} %get-tuple-element.32.mixed_ref, f32[16,128]{1,0:T(8,128)S(1)} %psum.15.squares_ref, bf16[1024,128]{1,0:T(8,128)(2,1)S(1)} %get-tuple-element.37.into_hi, ...), custom_call_target="tpu_custom_call" | custom-call | flops 134217728 | bytes 2097152 | tf_op jit(solution)/shard_map/pallas_call | solution.py:384
  59.2 8.7 %all-to-all-start.1 = ((f32[16,8,128]{2,1,0:T(8,128)}), f32[16,8,128]{2,1,0:T(8,128)S(1)}, u32[]{:S(2)}, u32[]{:S(2)}) async-start(f32[16,8,128]{2,1,0:T(8,128)} %get-tuple-element.42), calls=%async_computation.1 | async-start | bytes 131072 | tf_op jit(solution)/shard_map/all_to_all | solution.py:283
  67.8 1.6 %shard_map.96.within_ref = f32[1024,128]{1,0:T(8,128)S(1)} custom-call(f32[1024,128]{1,0:T(8,128)S(1)} %get-tuple-element.39.signal_ref, f32[64,128]{1,0:T(8,128)S(1)} %get-tuple-element.40.taps_ref), custom_call_target="tpu_custom_call" | custom-call | flops 536870912 | bytes 2097152 | tf_op jit(solution)/shard_map/pallas_call | solution.py:399
  69.5 2.7 %all-to-all-done.1.last_ref = f32[16,8,128]{2,1,0:T(8,128)S(1)} async-done(((f32[16,8,128]{2,1,0:T(8,128)}), f32[16,8,128]{2,1,0:T(8,128)S(1)}, u32[]{:S(2)}, u32[]{:S(2)}) %all-to-all-start.1) | async-done | bytes 65568 | tf_op jit(solution)/shard_map/all_to_all | solution.py:283
  72.1 1.1 %shard_map.97 = f32[64,2048]{1,0:T(8,128)} custom-call(s32[1]{0:T(128)} %bitcast.index_ref, f32[1024,128]{1,0:T(8,128)S(1)} %shard_map.96.within_ref, f32[1024,128]{1,0:T(8,128)S(1)} %get-tuple-element.41.states_ref, f32[16,8,128]{2,1,0:T(8,128)S(1)} %all-to-all-done.1.last_ref, bf16[1024,128]{1,0:T(8,128)(2,1)S(1)} %get-tuple-element.43.out_hi, ...), custom_call_target="tpu_custom_call" | custom-call | flops 134217728 | bytes 2097152 | tf_op jit(solution)/shard_map/pallas_call | solution.py:408
  (17 shorter events, 0.1 us)
Async XLA Ops:
  0.0 6.8 %copy-start.2 = (bf16[64,2048]{1,0:T(8,128)(2,1)S(1)}, bf16[64,2048]{1,0:T(8,128)(2,1)}, u32[]{:S(2)}) copy-start(bf16[64,2048]{1,0:T(8,128)(2,1)} %key_hbm.3) | copy-start | bytes 786436
  0.0 6.8 %copy-start.1 = (bf16[64,2048]{1,0:T(8,128)(2,1)S(1)}, bf16[64,2048]{1,0:T(8,128)(2,1)}, u32[]{:S(2)}) copy-start(bf16[64,2048]{1,0:T(8,128)(2,1)} %query_hbm.1) | copy-start | bytes 786436
  2.8 6.1 %collective-permute-start = (bf16[64,128]{1,0:T(8,128)(2,1)}, bf16[64,128]{1,0:T(8,128)(2,1)S(1)}, u32[]{:S(2)}, u32[]{:S(2)}) collective-permute-start(bf16[64,128]{1,0:T(8,128)(2,1)} %get-tuple-element.27), channel_id=1, source_target_pairs={{0,64},{64,128},{128,192},{192,256},{256,320},{320,384},{384,448},... | collective-permute-start | bytes 49160 | tf_op jit(solution)/shard_map/ppermute | solution.py:349
  6.8 0.7 copy-start.4
  7.5 1.0 %copy-start = (f32[1024,128]{1,0:T(8,128)S(1)}, f32[1024,128]{1,0:T(8,128)}, u32[]{:S(2)}) copy-start(f32[1024,128]{1,0:T(8,128)} %get-tuple-element.25.taps_ref) | copy-start | bytes 1572868
  23.2 20.1 %copy-start.5 = (f32[16,64]{1,0:T(8,128)S(1)}, f32[16,64]{1,0:T(8,128)}, u32[]{:S(2)}) copy-start(f32[16,64]{1,0:T(8,128)} %param.17) | copy-start | bytes 12292
  23.2 31.2 %all-to-all-start = ((bf16[32,8,128]{2,1,0:T(8,128)(2,1)}), bf16[32,8,128]{2,1,0:T(8,128)(2,1)S(1)}, u32[]{:S(2)}, u32[]{:S(2)}) async-start(bf16[32,8,128]{2,1,0:T(8,128)(2,1)} %broadcast_in_dim.4), calls=%async_computation | async-start | bytes 131072 | tf_op jit(solution)/shard_map/all_to_all | solution.py:283
  43.4 0.7 copy-start.6
  59.2 12.9 %all-to-all-start.1 = ((f32[16,8,128]{2,1,0:T(8,128)}), f32[16,8,128]{2,1,0:T(8,128)S(1)}, u32[]{:S(2)}, u32[]{:S(2)}) async-start(f32[16,8,128]{2,1,0:T(8,128)} %get-tuple-element.42), calls=%async_computation.1 | async-start | bytes 131072 | tf_op jit(solution)/shard_map/all_to_all | solution.py:283
  67.8 4.3 %copy-start.3 = (bf16[64,2048]{1,0:T(8,128)(2,1)S(1)}, bf16[64,2048]{1,0:T(8,128)(2,1)}, u32[]{:S(2)}) copy-start(bf16[64,2048]{1,0:T(8,128)(2,1)} %long_query_ref.1) | copy-start | bytes 786436
